TPU v7x, 32 devices: a whole 2x2x4 slice. The times are simulated.
32 devices in a mesh: tile: 8 (over y, x, core), lat: 4 (over z).
Axes of the slice: x: 2, y: 2, z: 4, core: 2. Of those that a mesh axis runs over, the one named last changes fastest.
Arguments:
- source: bfloat16 [224, 8, 4096], P(('tile', 'lat')), may hold values from -6 to 6
- row_map: bfloat16 [40, 8, 4, 32, 64], P('lat', 'tile'), may hold values from -0.375 to 0.375
- col_map: bfloat16 [40, 4, 64, 2560], P('lat', None, None, 'tile'), may hold values from -0.75 to 0.75
- pattern: int32 [40, 8, 4], P('lat', 'tile'), may hold values from 0 to 11, as said below
- codes: int32 [40, 8, 4], P('lat', 'tile'), may hold values from 0 to 3
- need_list: int32 [8, 4, 12], P('tile'), may hold values from 0 to 223, as said below
- owner: int32 [224], replicated, may hold values from 0 to 223, as said below
Outputs:
- spectrum: float32 [640, 16, 1281], P(('tile', 'lat'))
Inputs may be any that keep to these rules, and one draw needn't show every extreme that they name: need_list[t, l] names 12 distinct blocks, all held by devices of tile column t; each device that holds any of them holds exactly 3 of them. `owner`: a permutation of the slots. `pattern`: on each device every one of the 12 indices is used by some term.
All inputs are finite; a program needn't handle non-finite values.
Results may differ from a plain program's by a relative error of at most 0.0029.
Values may be sent and summed in bfloat16 or wider, within the bound.
A program may use at most 64 MiB of HBM per device.

v0:
```python
import math

import jax
import jax.numpy as jnp
from jax import lax
from jax.sharding import PartitionSpec as P

NLON = 2560
NLAT = 1280
M = 1280
NEED = 12
MOST = 3
LEV = 8


highest = lax.Precision.HIGHEST


def sectoral_logs():
    steps = jnp.arange(1, M, dtype=jnp.int32).astype(jnp.float32)
    terms = 0.5 * jnp.log1p(0.5 / steps)
    return jnp.concatenate([jnp.zeros((1,), jnp.float32), jnp.cumsum(terms)]) + 0.5 * math.log(0.5)


def legendre_sums(fields, pair_ids, colat, weights):
    count = pair_ids.shape[0]
    lats = colat.shape[0]
    norm_logs = sectoral_logs()
    orders = jnp.arange(M, dtype=jnp.int32)
    high_order = M - 1 - pair_ids
    low_length = M - pair_ids
    cosine = jnp.cos(colat)
    log_sine = jnp.log(jnp.sin(colat))

    def sectoral(order):
        picked = jnp.sum(
            jnp.where(order[:, None] == orders[None, :], norm_logs[None, :], 0.0), axis=1
        )
        exponent = picked[:, None] + order.astype(jnp.float32)[:, None] * log_sine[None, :]
        ramp = jnp.clip((exponent + 75.0) / 10.0, 0.0, 1.0)
        return jnp.exp(jnp.maximum(exponent, -75.0)) * ramp

    start_low = sectoral(pair_ids)
    start_high = sectoral(high_order)
    scaled = fields * weights[None, None, :, None]

    def advance(state, slot):
        previous, before = state
        is_low = slot < low_length
        order = jnp.where(is_low, pair_ids, high_order)
        degree = jnp.where(is_low, pair_ids + slot, high_order + slot - low_length)
        fresh = degree == order
        order_f = order.astype(jnp.float32)
        degree_f = degree.astype(jnp.float32)
        lower_f = degree_f - 1.0
        grows = degree > order
        ratio = jnp.where(
            grows,
            (4.0 * degree_f * degree_f - 1.0)
            / jnp.where(grows, degree_f * degree_f - order_f * order_f, 1.0),
            0.0,
        )
        back = degree - 1 > order
        inverse = jnp.where(
            back,
            (lower_f * lower_f - order_f * order_f)
            / jnp.where(back, 4.0 * lower_f * lower_f - 1.0, 1.0),
            0.0,
        )
        grown = jnp.sqrt(ratio)[:, None] * (
            cosine[None, :] * previous - jnp.sqrt(inverse)[:, None] * before
        )
        start = jnp.where(is_low[:, None], start_low, start_high)
        value = jnp.where(fresh[:, None], start, grown)
        return ((value, jnp.where(fresh[:, None], 0.0, previous)), value)

    def one_block(state, base):
        slots = base + jnp.arange(128, dtype=jnp.int32)
        state, table = lax.scan(advance, state, slots, unroll=8)
        low_mask = (slots[:, None] < low_length[None, :]).astype(jnp.float32)
        both = jnp.stack(
            [table * low_mask[:, :, None], table * (1.0 - low_mask)[:, :, None]], axis=2
        )
        sums = jnp.einsum("sqhl,qhlc->qcs", both, scaled, precision=highest)
        return (state, sums)

    zeros = jnp.zeros((count, lats), jnp.float32)
    total = -(-(M + 1) // 128)
    bases = jnp.arange(total, dtype=jnp.int32) * 128
    _, sums = lax.scan(one_block, (zeros, zeros), bases)
    sums = jnp.transpose(sums, (1, 2, 0, 3)).reshape(count, fields.shape[3], total * 128)
    return sums[:, :, : M + 1]


def row_products(picked, code, rmap, cmap):
    side = rmap.shape[2]
    blocks = picked.reshape(picked.shape[0], picked.shape[1], side, side)
    turned = jnp.swapaxes(blocks, 2, 3)
    chosen = jnp.where((code % 2 == 1)[:, None, None, None], turned, blocks)
    row_flip = (code == 1) | (code == 2)
    col_flip = (code == 2) | (code == 3)
    rmap = jnp.where(row_flip[:, None, None], rmap[:, :, ::-1], rmap)
    cmap = jnp.where(col_flip[:, None, None], cmap[:, ::-1, :], cmap)
    inner = jnp.einsum("klrc,kcx->klrx", chosen, cmap, preferred_element_type=jnp.float32).astype(
        jnp.bfloat16
    )
    return jnp.einsum("kar,klrx->lax", rmap, inner, preferred_element_type=jnp.float32)


def dft_table(base):
    columns = base + jnp.arange(256, dtype=jnp.int32)
    pair_index = columns // 4
    upper = columns // 2 % 2
    parity = columns % 2
    order = jnp.where(upper == 0, pair_index, M - 1 - pair_index)
    points = jnp.arange(NLON, dtype=jnp.int32)
    phase = points[:, None] * order[None, :] % NLON
    angle = phase.astype(jnp.float32) * (2.0 * math.pi / NLON)
    return jnp.where(parity[None, :] == 0, jnp.cos(angle), -jnp.sin(angle)) / math.sqrt(NLON)


def body(source, row_map, col_map, pattern, codes, need_list, owner):
    lat_count = lax.axis_size("lat")
    tile_count = lax.axis_size("tile")
    lat_me = lax.axis_index("lat")
    tile_me = lax.axis_index("tile")
    slots_dev = source.shape[0]
    block_ids = jnp.arange(owner.shape[0], dtype=jnp.int32)
    needs_column = need_list[0]
    holder = jnp.sum(
        jnp.where(needs_column[:, :, None] == block_ids[None, None, :], owner[None, None, :], 0),
        axis=2,
    )
    holder_lat = holder // slots_dev % lat_count
    holder_slot = holder % slots_dev
    my_lat = lax.dynamic_index_in_dim(holder_lat, lat_me, 0, keepdims=False)
    held_here = holder_lat == lat_me
    rank = jnp.cumsum(held_here.astype(jnp.int32), axis=1) - 1
    places = jnp.arange(MOST, dtype=jnp.int32)
    hit = held_here[:, None, :] & (rank[:, None, :] == places[None, :, None])
    picks = jnp.sum(jnp.where(hit, holder_slot[:, None, :], 0), axis=2)
    outgoing = jnp.take(source, picks.reshape(-1), axis=0).reshape(
        (lat_count, MOST) + source.shape[1:]
    )
    incoming = lax.all_to_all(outgoing, "lat", split_axis=0, concat_axis=0, tiled=True)
    earlier = jnp.arange(NEED)[:, None] > jnp.arange(NEED)[None, :]
    same = (my_lat[:, None] == my_lat[None, :]) & earlier
    my_rank = jnp.sum(same.astype(jnp.int32), axis=1)
    flat = incoming.reshape((lat_count * MOST,) + source.shape[1:])
    gathered = jnp.take(flat, my_lat * MOST + my_rank, axis=0)

    def one_row(inputs):
        index, code, rmap, cmap = inputs
        return row_products(jnp.take(gathered, index, axis=0), code, rmap, cmap)

    rows = lax.map(one_row, (pattern[:, 0], codes[:, 0], row_map[:, 0], col_map))
    field = jnp.transpose(rows, (1, 0, 2, 3)).reshape(
        rows.shape[1], rows.shape[0] * rows.shape[2], rows.shape[3]
    )
    lat_rows = lax.all_to_all(field, "tile", split_axis=1, concat_axis=2, tiled=True)
    levels = lat_rows.shape[0]
    count = lat_rows.shape[1]
    flat_rows = lat_rows.reshape(levels * count, NLON)

    def one_columns(base):
        return jnp.dot(flat_rows, dft_table(base), precision=highest)

    blocks = lax.map(one_columns, jnp.arange(2 * M // 256, dtype=jnp.int32) * 256)
    spectral = jnp.transpose(blocks, (1, 0, 2)).reshape(levels, count, 2 * M)
    arranged = lax.all_to_all(spectral, ("tile", "lat"), split_axis=2, concat_axis=1, tiled=True)
    pairs_dev = M // 2 // (lat_count * tile_count)
    spread_rows = NLAT // (lat_count * tile_count)
    positions = jnp.arange(NLAT, dtype=jnp.int32)
    group = positions // spread_rows
    latitude = (
        group % lat_count * (NLAT // lat_count)
        + group // lat_count * spread_rows
        + positions % spread_rows
    )
    colat = math.pi * (latitude.astype(jnp.float32) + 0.75) / (NLAT + 0.5)
    weights = math.pi * jnp.sin(colat) * math.sqrt(NLAT) / (NLAT + 0.5)
    fields = arranged.reshape(LEV, NLAT, pairs_dev, 2, 2)
    fields = jnp.transpose(fields, (2, 3, 1, 4, 0)).reshape(pairs_dev, 2, NLAT, 2 * LEV)
    pair_ids = (tile_me * lat_count + lat_me) * pairs_dev + jnp.arange(pairs_dev, dtype=jnp.int32)
    return legendre_sums(fields, pair_ids, colat, weights)


def solution(mesh):
    placed = (
        P(("tile", "lat"), None, None),
        P("lat", "tile", None, None, None),
        P("lat", None, None, "tile"),
        P("lat", "tile", None),
        P("lat", "tile", None),
        P("tile", None, None),
        P(),
    )
    return jax.shard_map(
        body, mesh=mesh, in_specs=placed, out_specs=P(("tile", "lat"), None, None), check_vma=False
    )
```

profile of v0, /device:TPU:1, one launch (start us, length us, event | category | flops | bytes accessed | tf_op | source)
XLA Modules:
  0.0 2540.4 jit_solution(5395046590276366607)
XLA Ops:
  30.2 61.6 %while.76 = (s32[]{:T(128)}, f32[10,8,32,320]{3,2,0,1:T(8,128)}, s32[10,4]{1,0:T(8,128)S(1)}, s32[10,4]{1,0:T(8,128)S(1)}, bf16[12,8,4096]{2,1,0:T(8,128)(2,1)S(...) while((s32[]{:T(128)}, f32[10,8,32,320]{3,2,0,1:T(8,128)}, ...), condition=%wide.region_9.10_spmd, body=%wide.region_8.9_spmd.sunk | while | flops 126968936 | bytes 4151017 | solution.py:156
  104.1 42.7 %all-to-all-done.1 = f32[8,320,320]{2,0,1:T(8,128)} async-done(((f32[8,320,320]{2,0,1:T(8,128)}), f32[8,320,320]{2,0,1:T(8,128)}, u32[]{:S(2)}, u32[]{:S(2)}) %all-to-all-start.1) | async-done | bytes 3276832 | tf_op jit(solution)/shard_map/all_to_all | solution.py:160
  158.0 202.3 %while.77 = (s32[]{:T(128)}, f32[10,320,256]{2,1,0:T(8,128)}, s32[10]{0:T(128)S(1)}, f32[320,2560]{1,0:T(8,128)}, s32[]{:T(128)}) while((s32[]{:T(128)}, f32[10,320,256]{2,1,0:T(8,128)}, s32[10]{0:T(128)S(1)}, f32[320,2560]{1,0:T(8,128)}, s32[]{:T(128)}) %tuple.253), condition=%wide.region_11.12_spmd, body=%wide.region_10.11_spmd.sunk | while | flops 2524460288 | bytes 3607633 | solution.py:168
  395.1 72.0 %all-to-all-done.2 = f32[32,1,25600]{2,1,0:T(1,128)} async-done(((f32[32,1,25600]{2,1,0:T(1,128)}), f32[32,1,25600]{2,1,0:T(1,128)}, u32[]{:S(2)}, u32[]{:S(2)}) %all-to-all-start.2) | async-done | bytes 3276832 | tf_op jit(solution)/shard_map/all_to_all | solution.py:170
  519.1 2019.7 %while.79 = (s32[]{:T(128)}, f32[20,1280]{1,0:T(8,128)S(1)}, f32[20,1280]{1,0:T(8,128)S(1)}, f32[11,20,16,128]{3,2,1,0:T(8,128)S(1)}, s32[11]{0:T(128)S(1)}, /*i...) while((s32[]{:T(128)}, f32[20,1280]{1,0:T(8,128)S(1)}, ...), condition=%wide.region_15.16_spmd.clone.clone.clone, body=%wide.region_12.15_spmd.clone.clone.clone.sunk | while | flops 1277916544 | bytes 89526456 | solution.py:90
  520.9 152.7 %while.80 = (s32[]{:T(128)}, f32[20,1280]{1,0:T(8,128)S(1)}, f32[20,1280]{1,0:T(8,128)S(1)}, f32[16,8,20,1280]{3,1,0,2:T(8,128)}, s32[16,8]{0,1:T(8,128)S(1)}, /...) while((s32[]{:T(128)}, f32[20,1280]{1,0:T(8,128)S(1)}, ...), condition=%wide.region_14.14_spmd.clone, body=%wide.region_13.13_spmd.clone.sunk | while | flops 6097681 | bytes 7183545 | solution.py:79
  680.6 22.3 fusion.258
  704.5 152.7 %while.80 = (s32[]{:T(128)}, f32[20,1280]{1,0:T(8,128)S(1)}, f32[20,1280]{1,0:T(8,128)S(1)}, f32[16,8,20,1280]{3,1,0,2:T(8,128)}, s32[16,8]{0,1:T(8,128)S(1)}, /...) while((s32[]{:T(128)}, f32[20,1280]{1,0:T(8,128)S(1)}, ...), condition=%wide.region_14.14_spmd.clone, body=%wide.region_13.13_spmd.clone.sunk | while | flops 6097681 | bytes 7183545 | solution.py:79
  864.2 22.3 fusion.258
  888.1 152.7 %while.80 = (s32[]{:T(128)}, f32[20,1280]{1,0:T(8,128)S(1)}, f32[20,1280]{1,0:T(8,128)S(1)}, f32[16,8,20,1280]{3,1,0,2:T(8,128)}, s32[16,8]{0,1:T(8,128)S(1)}, /...) while((s32[]{:T(128)}, f32[20,1280]{1,0:T(8,128)S(1)}, ...), condition=%wide.region_14.14_spmd.clone, body=%wide.region_13.13_spmd.clone.sunk | while | flops 6097681 | bytes 7183545 | solution.py:79
  1047.8 22.3 fusion.258
  1071.7 152.7 %while.80 = (s32[]{:T(128)}, f32[20,1280]{1,0:T(8,128)S(1)}, f32[20,1280]{1,0:T(8,128)S(1)}, f32[16,8,20,1280]{3,1,0,2:T(8,128)}, s32[16,8]{0,1:T(8,128)S(1)}, /...) while((s32[]{:T(128)}, f32[20,1280]{1,0:T(8,128)S(1)}, ...), condition=%wide.region_14.14_spmd.clone, body=%wide.region_13.13_spmd.clone.sunk | while | flops 6097681 | bytes 7183545 | solution.py:79
  1231.4 22.3 fusion.258
  1255.3 152.7 %while.80 = (s32[]{:T(128)}, f32[20,1280]{1,0:T(8,128)S(1)}, f32[20,1280]{1,0:T(8,128)S(1)}, f32[16,8,20,1280]{3,1,0,2:T(8,128)}, s32[16,8]{0,1:T(8,128)S(1)}, /...) while((s32[]{:T(128)}, f32[20,1280]{1,0:T(8,128)S(1)}, ...), condition=%wide.region_14.14_spmd.clone, body=%wide.region_13.13_spmd.clone.sunk | while | flops 6097681 | bytes 7183545 | solution.py:79
  1415.0 22.3 fusion.258
  1438.9 152.7 %while.80 = (s32[]{:T(128)}, f32[20,1280]{1,0:T(8,128)S(1)}, f32[20,1280]{1,0:T(8,128)S(1)}, f32[16,8,20,1280]{3,1,0,2:T(8,128)}, s32[16,8]{0,1:T(8,128)S(1)}, /...) while((s32[]{:T(128)}, f32[20,1280]{1,0:T(8,128)S(1)}, ...), condition=%wide.region_14.14_spmd.clone, body=%wide.region_13.13_spmd.clone.sunk | while | flops 6097681 | bytes 7183545 | solution.py:79
  1598.5 22.3 fusion.258
  1622.5 152.7 %while.80 = (s32[]{:T(128)}, f32[20,1280]{1,0:T(8,128)S(1)}, f32[20,1280]{1,0:T(8,128)S(1)}, f32[16,8,20,1280]{3,1,0,2:T(8,128)}, s32[16,8]{0,1:T(8,128)S(1)}, /...) while((s32[]{:T(128)}, f32[20,1280]{1,0:T(8,128)S(1)}, ...), condition=%wide.region_14.14_spmd.clone, body=%wide.region_13.13_spmd.clone.sunk | while | flops 6097681 | bytes 7183545 | solution.py:79
  1782.1 22.3 fusion.258
  1806.1 152.7 %while.80 = (s32[]{:T(128)}, f32[20,1280]{1,0:T(8,128)S(1)}, f32[20,1280]{1,0:T(8,128)S(1)}, f32[16,8,20,1280]{3,1,0,2:T(8,128)}, s32[16,8]{0,1:T(8,128)S(1)}, /...) while((s32[]{:T(128)}, f32[20,1280]{1,0:T(8,128)S(1)}, ...), condition=%wide.region_14.14_spmd.clone, body=%wide.region_13.13_spmd.clone.sunk | while | flops 6097681 | bytes 7183545 | solution.py:79
  1965.7 22.3 fusion.258
  1989.6 152.7 %while.80 = (s32[]{:T(128)}, f32[20,1280]{1,0:T(8,128)S(1)}, f32[20,1280]{1,0:T(8,128)S(1)}, f32[16,8,20,1280]{3,1,0,2:T(8,128)}, s32[16,8]{0,1:T(8,128)S(1)}, /...) while((s32[]{:T(128)}, f32[20,1280]{1,0:T(8,128)S(1)}, ...), condition=%wide.region_14.14_spmd.clone, body=%wide.region_13.13_spmd.clone.sunk | while | flops 6097681 | bytes 7183545 | solution.py:79
  2173.2 152.7 %while.80 = (s32[]{:T(128)}, f32[20,1280]{1,0:T(8,128)S(1)}, f32[20,1280]{1,0:T(8,128)S(1)}, f32[16,8,20,1280]{3,1,0,2:T(8,128)}, s32[16,8]{0,1:T(8,128)S(1)}, /...) while((s32[]{:T(128)}, f32[20,1280]{1,0:T(8,128)S(1)}, ...), condition=%wide.region_14.14_spmd.clone, body=%wide.region_13.13_spmd.clone.sunk | while | flops 6097681 | bytes 7183545 | solution.py:79
  2356.8 152.7 %while.80 = (s32[]{:T(128)}, f32[20,1280]{1,0:T(8,128)S(1)}, f32[20,1280]{1,0:T(8,128)S(1)}, f32[16,8,20,1280]{3,1,0,2:T(8,128)}, s32[16,8]{0,1:T(8,128)S(1)}, /...) while((s32[]{:T(128)}, f32[20,1280]{1,0:T(8,128)S(1)}, ...), condition=%wide.region_14.14_spmd.clone, body=%wide.region_13.13_spmd.clone.sunk | while | flops 6097681 | bytes 7183545 | solution.py:79
  (3722 shorter events, 2227.0 us)
Async XLA Ops:
  0.0 2.7 copy-start
  0.0 9.7 copy-start.3
  0.0 9.8 copy-start.4
  4.3 25.1 all-to-all-start
  98.1 48.8 %all-to-all-start.1 = ((f32[8,320,320]{2,0,1:T(8,128)}), f32[8,320,320]{2,0,1:T(8,128)}, u32[]{:S(2)}, u32[]{:S(2)}) async-start(f32[8,320,320]{2,0,1:T(8,128)} %copy.77), calls=%async_computation.1 | async-start | bytes 7864320 | tf_op jit(solution)/shard_map/all_to_all | solution.py:160
  387.3 79.8 %all-to-all-start.2 = ((f32[32,1,25600]{2,1,0:T(1,128)}), f32[32,1,25600]{2,1,0:T(1,128)}, u32[]{:S(2)}, u32[]{:S(2)}) async-start(f32[32,1,25600]{2,1,0:T(1,128)} %reshape.1094), calls=%async_computation.2 | async-start | bytes 6553600 | tf_op jit(solution)/shard_map/all_to_all | solution.py:170
  674.4 6.1 copy-start.2
  858.0 6.1 copy-start.2
  1041.6 6.1 copy-start.2
  1225.2 6.1 copy-start.2
  1408.8 6.1 copy-start.2
  1592.4 6.1 copy-start.2
  1776.0 6.1 copy-start.2
  1959.6 6.1 copy-start.2
  2143.2 6.1 copy-start.2
  2326.8 6.1 copy-start.2
  2510.4 6.1 copy-start.2
  2538.8 1.4 copy-start.1
where the time goes:
time: 2570 us; the launch traced here: 2540 us
  other arithmetic  1450 us (56%)
  local copies, waits for them, and re-layouts  461 us (18%)
  matrix products  456 us (18%)
  waiting for transfers between devices  134 us (5%)
    lt x176, other arithmetic, advance(): is_low = slot < low_length  855 us
    while x1232, other arithmetic  282 us
    dot_general x11, matrix products, one_block(): sums = jnp.einsum('sqhl,qhlc->qcs', both, scaled, precision=highest)  245 us
    dynamic_update_slice x176, local copies, waits for them, and re-layouts, one_block(): state, table = lax.scan(advance, state, slots, unroll=8)  207 us
    dot_general x10, matrix products, one_columns(): return jnp.dot(flat_rows, dft_table(base), precision=highest)  185 us
    sqrt x880, other arithmetic, advance(): jnp.sqrt(ratio)[:, None]  118 us
    slice x176, local copies, waits for them, and re-layouts, one_block(): state, table = lax.scan(advance, state, slots, unroll=8)  110 us
    all_to_all x1, waiting for transfers between devices, body(): lax.all_to_all(spectral, ('tile', 'lat'), split_axis=2, concat_axis=1, ti...  72 us
  transfers between devices with their start and end apart: 3, of which 3 were waited for; matrix products, arithmetic and copies ran while one was open for 0% of the time, Pallas kernels for 0%

commit v1 on v0

v1 whole, which is shorter than its diff:
```python
import math

import jax
import jax.numpy as jnp
from jax import lax
from jax.experimental import pallas as pl
from jax.experimental.pallas import tpu as pltpu
from jax.sharding import PartitionSpec as P

NLON = 2560
NLAT = 1280
M = 1280
HALF = NLAT // 2
NEED = 12
MOST = 3
LEV = 8
BS = 64
RB = 32
K = 4
QB = 64
SB = 128
SCALE = 1024.0


def permutation(size, flip):
    rows = lax.broadcasted_iota(jnp.int32, (size, size), 0)
    cols = lax.broadcasted_iota(jnp.int32, (size, size), 1)
    target = jnp.where(flip, size - 1 - cols, cols)
    return jnp.where(rows == target, 1.0, 0.0).astype(jnp.bfloat16)


def regrid_kernel(pos, code, south, blocks, rmap, cmap, out, inner, rall):
    g = pl.program_id(0)
    turn = permutation(RB, south[0] == 1)
    for k in range(K):
        c = code[g * K + k]
        where = pos[g * K + k] + NEED * (c % 2)
        picked = blocks[where]
        cols = jnp.dot(permutation(BS, c >= 2), cmap[0, k], preferred_element_type=jnp.float32)
        prod = jnp.dot(picked, cols.astype(jnp.bfloat16), preferred_element_type=jnp.float32)
        inner[:, k * BS : (k + 1) * BS, :] = prod.astype(jnp.bfloat16).reshape(LEV, BS, -1)
        flip = (c == 1) | (c == 2)
        rows = jnp.dot(rmap[0, 0, k], permutation(BS, flip), preferred_element_type=jnp.float32)
        rows = jnp.dot(turn, rows.astype(jnp.bfloat16), preferred_element_type=jnp.float32)
        rall[:, k * BS : (k + 1) * BS] = rows.astype(jnp.bfloat16)
    for lev in range(LEV):
        out[lev] = jnp.dot(rall[...], inner[lev], preferred_element_type=jnp.float32).astype(
            jnp.bfloat16
        )


def regrid(blocks, rmap, cmap, pos, code, south):
    bands = cmap.shape[0]
    width = cmap.shape[3]

    def out_map(g, pos, code, south):
        return (0, jnp.where(south[0] == 1, bands - 1 - g, g), 0)

    return pl.pallas_call(
        regrid_kernel,
        out_shape=jax.ShapeDtypeStruct((LEV, bands * RB, width), jnp.bfloat16),
        grid_spec=pltpu.PrefetchScalarGridSpec(
            num_scalar_prefetch=3,
            grid=(bands,),
            in_specs=[
                pl.BlockSpec(blocks.shape, lambda g, *_: (0, 0, 0)),
                pl.BlockSpec((1, 1, K, RB, BS), lambda g, *_: (g, 0, 0, 0, 0)),
                pl.BlockSpec((1, K, BS, width), lambda g, *_: (g, 0, 0, 0)),
            ],
            out_specs=pl.BlockSpec((LEV, RB, width), out_map),
            scratch_shapes=[
                pltpu.VMEM((LEV, K * BS, width), jnp.bfloat16),
                pltpu.VMEM((RB, K * BS), jnp.bfloat16),
            ],
        ),
        name="regrid",
    )(pos, code, south, blocks, rmap, cmap)


def dft_kernel(rows, base_cos, base_sin, step_cos, step_sin, out, high, low):
    bc = base_cos[...]
    bs = base_sin[...]
    for kind in range(4):
        ca = step_cos[0, kind // 2 : kind // 2 + 1, :]
        sa = step_sin[0, kind // 2 : kind // 2 + 1, :]
        if kind == 0:
            w = ca * bc - sa * bs
        elif kind == 1:
            w = -(sa * bc + ca * bs)
        elif kind == 2:
            w = ca * bc + sa * bs
        else:
            w = ca * bs - sa * bc
        top = w.astype(jnp.bfloat16)
        high[kind * QB : (kind + 1) * QB, :] = top
        low[kind * QB : (kind + 1) * QB, :] = (w - top.astype(jnp.float32)).astype(jnp.bfloat16)
    dims = (((1,), (1,)), ((), ()))
    total = lax.dot_general(high[...], rows[...], dims, preferred_element_type=jnp.float32)
    total += lax.dot_general(low[...], rows[...], dims, preferred_element_type=jnp.float32)
    total = total * (1.0 / math.sqrt(NLON))
    for kind in range(4):
        out[kind] = total[kind * QB : (kind + 1) * QB, :].astype(jnp.bfloat16)


def turns(orders):
    points = jnp.arange(NLON, dtype=jnp.int32)
    phase = orders[..., None] * points % NLON
    angle = phase.astype(jnp.float32) * (2.0 * math.pi / NLON)
    return jnp.cos(angle), jnp.sin(angle)


def dft(rows, tables):
    base_cos, base_sin, step_cos, step_sin = tables
    count = rows.shape[0]
    steps = M // 2 // QB
    return pl.pallas_call(
        dft_kernel,
        out_shape=jax.ShapeDtypeStruct((4, M // 2, count), jnp.bfloat16),
        grid=(steps,),
        in_specs=[
            pl.BlockSpec((count, NLON), lambda j: (0, 0)),
            pl.BlockSpec((QB, NLON), lambda j: (0, 0)),
            pl.BlockSpec((QB, NLON), lambda j: (0, 0)),
            pl.BlockSpec((1, 2, NLON), lambda j: (j, 0, 0)),
            pl.BlockSpec((1, 2, NLON), lambda j: (j, 0, 0)),
        ],
        out_specs=pl.BlockSpec((4, QB, count), lambda j: (0, j, 0)),
        scratch_shapes=[
            pltpu.VMEM((4 * QB, NLON), jnp.bfloat16),
            pltpu.VMEM((4 * QB, NLON), jnp.bfloat16),
        ],
        name="dft",
    )(rows, base_cos, base_sin, step_cos, step_sin)


def dft_tables():
    base = turns(jnp.arange(QB, dtype=jnp.int32))
    first = jnp.arange(M // 2 // QB, dtype=jnp.int32) * QB
    step = turns(jnp.stack([first, M - 1 - first], axis=1))
    return base + step


def legendre_kernel(
    first, fields, x_ref, start_low, start_high, grow, back, out, table, prev_ref, before_ref
):
    pairs = out.shape[0]
    padded = start_low.shape[0]
    first_pair = first[0]
    x = x_ref[...]
    fresh_last = M - first_pair
    fresh_first = fresh_last - padded + 1

    def eight(prev, before, a8, b8, slot, row, careful):
        for k in range(8):
            value = a8[:, k : k + 1] * (x * prev) - b8[:, k : k + 1] * before
            if careful:
                pair = lax.broadcasted_iota(jnp.int32, prev.shape, 0) + first_pair
                value = jnp.where(pair + (slot + k) == M, start_high[...], value)
                value = jnp.where(slot + k == 0, start_low[...], value)
            for lane in range(HALF // 128):
                table[lane, pl.ds(row + k * padded, padded), :] = value[
                    :, lane * 128 : (lane + 1) * 128
                ]
            prev, before = value, prev
        return prev, before

    def block(slot0, count):
        a_block = grow[:, pl.ds(slot0, SB)]
        b_block = back[:, pl.ds(slot0, SB)]

        def some(i, carry):
            prev, before, a8, b8 = carry
            slot = slot0 + i * 8
            row = pl.multiple_of(i * 8 * padded, 8)
            careful = (slot == 0) | ((slot + 7 >= fresh_first) & (slot <= fresh_last))
            prev, before = lax.cond(
                careful,
                lambda p, b: eight(p, b, a8, b8, slot, row, True),
                lambda p, b: eight(p, b, a8, b8, slot, row, False),
                prev,
                before,
            )
            return prev, before, pltpu.roll(a8, SB - 8, 1), pltpu.roll(b8, SB - 8, 1)

        carry = (prev_ref[...], before_ref[...], a_block, b_block)
        prev, before, _, _ = lax.fori_loop(0, count // 8, some, carry)
        prev_ref[...] = prev
        before_ref[...] = before

        @pl.loop(0, pairs)
        def _(q):
            lanes = [
                table[lane, pl.ds(q, count, stride=padded), :] for lane in range(HALF // 128)
            ]
            p32 = jnp.concatenate(lanes, axis=1)
            high = p32.astype(jnp.bfloat16)
            low = (p32 - high.astype(jnp.float32)).astype(jnp.bfloat16)
            dims = (((1,), (1,)), ((), ()))
            field = fields[q]
            sums = lax.dot_general(high, field, dims, preferred_element_type=jnp.float32)
            sums += lax.dot_general(low, field, dims, preferred_element_type=jnp.float32)
            sums = sums.T
            slots = lax.broadcasted_iota(jnp.int32, (2 * LEV, count), 1) + slot0
            length = M - first_pair - q
            is_low = slots < length
            odd = jnp.where(is_low, slots, slots + length) % 2
            sign = jnp.where(odd == 1, -1.0, 1.0)
            c = 2 * LEV
            north = jnp.where(is_low, sums[0:c], sums[2 * c : 3 * c])
            southern = jnp.where(is_low, sums[c : 2 * c], sums[3 * c : 4 * c])
            result = (north + sign * southern) * (1.0 / SCALE)
            if count == SB:
                out[q, :, pl.ds(slot0, SB)] = result
            else:
                out[q, :, M : M + 1] = result[:, 0:1]

    prev_ref[...] = jnp.zeros_like(prev_ref)
    before_ref[...] = jnp.zeros_like(before_ref)

    @pl.loop(0, M // SB)
    def _(b):
        block(pl.multiple_of(b * SB, SB), SB)

    block(M, 8)


def legendre(fields, tables, first):
    x, start_low, start_high, grow, back = tables
    pairs = fields.shape[0]
    padded = start_low.shape[0]
    vmem = pl.BlockSpec(memory_space=pltpu.VMEM)
    return pl.pallas_call(
        legendre_kernel,
        out_shape=jax.ShapeDtypeStruct((pairs, 2 * LEV, M + 1), jnp.float32),
        in_specs=[pl.BlockSpec(memory_space=pltpu.SMEM)] + [vmem] * 6,
        out_specs=vmem,
        scratch_shapes=[
            pltpu.VMEM((HALF // 128, SB * padded, 128), jnp.float32),
            pltpu.VMEM((padded, HALF), jnp.float32),
            pltpu.VMEM((padded, HALF), jnp.float32),
        ],
        name="legendre",
    )(first, fields, x, start_low, start_high, grow, back)


def legendre_tables(first, pairs):
    padded = -(-pairs // 8) * 8
    pair_ids = first + jnp.arange(padded, dtype=jnp.int32)
    latitude = jnp.arange(HALF, dtype=jnp.int32).astype(jnp.float32)
    colat = math.pi * (latitude + 0.75) / (NLAT + 0.5)
    weights = math.pi * jnp.sin(colat) * math.sqrt(NLAT) / (NLAT + 0.5)
    cosine = jnp.cos(colat)
    log_sine = jnp.log(jnp.sin(colat))
    steps = jnp.arange(1, M, dtype=jnp.int32).astype(jnp.float32)
    terms = 0.5 * jnp.log1p(0.5 / steps)
    norm_logs = jnp.concatenate([jnp.zeros((1,), jnp.float32), jnp.cumsum(terms)])
    norm_logs = norm_logs + 0.5 * math.log(0.5)
    orders = jnp.arange(M, dtype=jnp.int32)
    high_order = M - 1 - pair_ids
    low_length = (M - pair_ids)[:, None]

    def sectoral(order):
        picked = jnp.sum(
            jnp.where(order[:, None] == orders[None, :], norm_logs[None, :], 0.0), axis=1
        )
        exponent = picked[:, None] + order.astype(jnp.float32)[:, None] * log_sine[None, :]
        ramp = jnp.clip((exponent + 75.0) / 10.0, 0.0, 1.0)
        value = jnp.exp(jnp.maximum(exponent, -75.0)) * ramp
        return value * (weights * SCALE)[None, :]

    slot = jnp.arange(M + SB, dtype=jnp.int32)[None, :]
    is_low = slot < low_length
    order = jnp.where(is_low, pair_ids[:, None], high_order[:, None])
    degree = order + jnp.where(is_low, slot, slot - low_length)
    order_f = order.astype(jnp.float32)
    degree_f = degree.astype(jnp.float32)
    lower_f = degree_f - 1.0
    grows = degree > order
    ratio = jnp.where(
        grows,
        (4.0 * degree_f * degree_f - 1.0)
        / jnp.where(grows, degree_f * degree_f - order_f * order_f, 1.0),
        0.0,
    )
    behind = degree - 1 > order
    inverse = jnp.where(
        behind,
        (lower_f * lower_f - order_f * order_f)
        / jnp.where(behind, 4.0 * lower_f * lower_f - 1.0, 1.0),
        0.0,
    )
    grow = jnp.sqrt(ratio)
    back = grow * jnp.sqrt(inverse)
    return cosine[None, :], sectoral(pair_ids), sectoral(high_order), grow, back


def body(source, row_map, col_map, pattern, codes, need_list, owner):
    lat_count = lax.axis_size("lat")
    tile_count = lax.axis_size("tile")
    lat_me = lax.axis_index("lat")
    tile_me = lax.axis_index("tile")
    slots_dev = source.shape[0]
    block_ids = jnp.arange(owner.shape[0], dtype=jnp.int32)
    needs_column = need_list[0]
    holder = jnp.sum(
        jnp.where(needs_column[:, :, None] == block_ids[None, None, :], owner[None, None, :], 0),
        axis=2,
    )
    holder_lat = holder // slots_dev % lat_count
    holder_slot = holder % slots_dev
    my_lat = lax.dynamic_index_in_dim(holder_lat, lat_me, 0, keepdims=False)
    held_here = holder_lat == lat_me
    rank = jnp.cumsum(held_here.astype(jnp.int32), axis=1) - 1
    places = jnp.arange(MOST, dtype=jnp.int32)
    hit = held_here[:, None, :] & (rank[:, None, :] == places[None, :, None])
    picks = jnp.sum(jnp.where(hit, holder_slot[:, None, :], 0), axis=2)
    outgoing = jnp.take(source, picks.reshape(-1), axis=0).reshape(
        (lat_count, MOST) + source.shape[1:]
    )
    incoming = lax.all_to_all(outgoing, "lat", split_axis=0, concat_axis=0, tiled=True)
    earlier = jnp.arange(NEED)[:, None] > jnp.arange(NEED)[None, :]
    same = (my_lat[:, None] == my_lat[None, :]) & earlier
    my_rank = jnp.sum(same.astype(jnp.int32), axis=1)
    place = my_lat * MOST + my_rank
    flat = incoming.reshape(lat_count * MOST, LEV, BS, BS)
    return place, flat


def whole(source, row_map, col_map, pattern, codes, need_list, owner):
    lat_count = lax.axis_size("lat")
    tile_count = lax.axis_size("tile")
    lat_me = lax.axis_index("lat")
    tile_me = lax.axis_index("tile")
    place, flat = body(source, row_map, col_map, pattern, codes, need_list, owner)
    held = flat.shape[0]
    uses = pattern[:, 0].reshape(-1)
    wanted = jnp.arange(NEED, dtype=jnp.int32)
    pos = jnp.sum(jnp.where(uses[:, None] == wanted[None, :], place[None, :], 0), axis=1)
    code = codes[:, 0].reshape(-1)
    pos = pos + (held - NEED) * (code % 2)
    blocks = jnp.concatenate([flat, jnp.swapaxes(flat, 2, 3)]).reshape(2 * held, LEV * BS, BS)
    south = (lat_me >= lat_count // 2).astype(jnp.int32).reshape(1)
    field = regrid(blocks, row_map, col_map, pos, code, south)

    flat_rows = field.reshape(LEV * field.shape[1], field.shape[2])
    rows = lax.all_to_all(flat_rows, "tile", split_axis=0, concat_axis=1, tiled=True)
    spectral = dft(rows, dft_tables())
    arranged = lax.all_to_all(spectral, ("tile", "lat"), split_axis=1, concat_axis=0, tiled=True)

    parts = tile_count // LEV
    pairs = M // 2 // (tile_count * lat_count)
    count = rows.shape[0]
    box = arranged.reshape(LEV, parts, lat_count, 2, 2, pairs, count)
    halves = lat_count // 2
    north = box[:, :, :halves]
    southern = box[:, :, halves:][:, :, ::-1]
    both = jnp.stack([north, southern])
    fields = jnp.transpose(both, (6, 4, 0, 5, 1, 3, 2, 7)).reshape(pairs, 8 * LEV, HALF)
    first = (tile_me * lat_count + lat_me) * pairs
    return legendre(fields, legendre_tables(first, pairs), first.reshape(1))


def solution(mesh):
    placed = (
        P(("tile", "lat"), None, None),
        P("lat", "tile", None, None, None),
        P("lat", None, None, "tile"),
        P("lat", "tile", None),
        P("lat", "tile", None),
        P("tile", None, None),
        P(),
    )
    return jax.shard_map(
        whole, mesh=mesh, in_specs=placed, out_specs=P(("tile", "lat"), None, None), check_vma=False
    )
```

time: 2570 us -> 298 us (0.12); the launches traced: 2540 us -> 297 us
  other arithmetic: 1450 us -> 21.2 us
  matrix products: 456 us -> 0 us
  local copies, waits for them, and re-layouts: 461 us -> 34.8 us
  Pallas kernels: 0 us -> 152 us
  waiting for transfers between devices: 134 us -> 73.1 us
    lt x176 -> x0, other arithmetic: 855 us -> none  [advance(): is_low = slot < low_length]
    dot_general x31 -> x0, matrix products: 456 us -> none  [the longest x11 245 us: one_block(): sums = jnp.einsum('sqhl,qhlc->qcs', both, scaled, precision=highest)]
    while x1232 -> x0, other arithmetic: 282 us -> none
    dynamic_update_slice x176 -> x0, local copies, waits for them, and re-layouts: 207 us -> none  [one_block(): state, table = lax.scan(advance, state, slots, unroll=8)]
    pallas_call x0 -> x3, Pallas kernels: none -> 152 us  [the longest x1 111 us: legendre(): pl.pallas_call(legendre_kernel, out_shape=jax.ShapeDtypeStruct((pairs, 2...]
    sqrt x880 -> x0, other arithmetic: 118 us -> none  [advance(): jnp.sqrt(ratio)[:, None]]
    slice x177 -> x2, local copies, waits for them, and re-layouts: 110 us -> 2.66 us  [the longest x1 2.58 us: whole(): north = box[:, :, :halves]]
    mul x26 -> x5, other arithmetic: 73 us -> 1.82 us  [the longest x1 0.98 us: legendre_tables(): back = grow * jnp.sqrt(inverse)]
  transfers between devices with their start and end apart: 3 -> 3, of which waited for: 3 -> 3; matrix products, arithmetic and copies ran while one was open for 0% -> 5% of each run, Pallas kernels for 0% -> 0%
where the time goes in v1:
time: 298 us; the launch traced here: 297 us
  Pallas kernels  152 us (51%)
  waiting for transfers between devices  73.1 us (25%)
  local copies, waits for them, and re-layouts  34.8 us (12%)
  other arithmetic  21.2 us (7%)
  starting transfers between devices  16.3 us (5%)
    pallas_call x1, Pallas kernels, legendre(): pl.pallas_call(legendre_kernel, out_shape=jax.ShapeDtypeStruct((pairs, 2...  111 us
    all_to_all x1, waiting for transfers between devices, whole(): lax.all_to_all(spectral, ('tile', 'lat'), split_axis=1, concat_axis=0, ti...  42.3 us
    pallas_call x1, Pallas kernels, regrid(): pl.pallas_call(regrid_kernel, out_shape=jax.ShapeDtypeStruct((LEV, bands...  22.8 us
    pallas_call x1, Pallas kernels, dft(): pl.pallas_call(dft_kernel, out_shape=jax.ShapeDtypeStruct((4, M // 2, cou...  18 us
    all_to_all x1, waiting for transfers between devices, body(): lax.all_to_all(outgoing, 'lat', split_axis=0, concat_axis=0, tiled=True)  17.4 us
    all_to_all x1, waiting for transfers between devices, whole(): lax.all_to_all(flat_rows, 'tile', split_axis=0, concat_axis=1, tiled=True)  13.4 us
    sin x2, other arithmetic, turns(): return (jnp.cos(angle), jnp.sin(angle))  8.27 us
  transfers between devices with their start and end apart: 3, of which 3 were waited for; matrix products, arithmetic and copies ran while one was open for 5% of the time, Pallas kernels for 0%

profile of v1, /device:TPU:1, one launch (start us, length us, event | category | flops | bytes accessed | tf_op | source)
XLA Modules:
  0.0 297.1 jit_solution(13382954942386132781)
XLA Ops:
  4.4 5.4 %all-to-all-start = ((bf16[4,3,8,4096]{3,2,1,0:T(8,128)(2,1)}), bf16[4,3,8,4096]{3,2,1,0:T(8,128)(2,1)S(1)}, u32[]{:S(2)}, u32[]{:S(2)}) async-start(bf16[4,3,8,4096]{3,2,1,0:T(8,128)(2,1)} %broadcast_select_fusion), calls=%async_computation | async-start | bytes 1572864 | tf_op jit(solution)/shard_map/all_to_all | solution.py:320
  12.0 17.4 %all-to-all-done = bf16[4,3,8,4096]{3,2,1,0:T(8,128)(2,1)S(1)} async-done(((bf16[4,3,8,4096]{3,2,1,0:T(8,128)(2,1)}), bf16[4,3,8,4096]{3,2,1,0:T(8,128)(2,1)S(1)}, u32[]{:S(2)}, u32[]{:S(2)}) %all-to-all-start) | async-done | bytes 786464 | tf_op jit(solution)/shard_map/all_to_all | solution.py:320
  29.4 1.7 reshape.215
  31.1 1.6 copy.52
  32.7 2.6 concatenate.17
  35.3 3.7 %pad_maximum_fusion.blocks = bf16[24,512,64]{2,1,0:T(8,128)(2,1)} fusion(bf16[12,512,64]{2,1,0:T(8,128)(2,1)S(1)} %bitcast.39, bf16[12,512,64]{2,1,0:T(8,128)(2,1)} %concatenate.17), kind=kLoop, calls=%fused_computation.1 | loop fusion | flops 786432 | bytes 3145728 | tf_op jit(solution)/shard_map/concatenate | solution.py:341
  39.0 22.8 %regrid.1 = bf16[8,320,320]{2,1,0:T(8,128)(2,1)} custom-call(s32[40]{0:T(128)} %select_reduce_fusion.3.pos, s32[40]{0:T(128)} %reshape_squeeze.3.code, s32[1]{0:T(128)} %bitcast.3.south, bf16[24,512,64]{2,1,0:T(8,128)(2,1)} %pad_maximum_fusion.blocks, bf16[10,1,4,32,64]{4,3,2,1,0:T(8,128)(2,1)} %rmap.1, bf16[10,4,64,320]{3,2,1,0:T(8,128)(2,1)} %cmap.1), custom_call_target="tpu_custom_call" | custom-call | tf_op jit(solution)/shard_map/regrid/pallas_call | solution.py:59
  61.9 5.1 %all-to-all-start.1 = ((bf16[8,320,320]{2,1,0:T(8,128)(2,1)}), bf16[8,320,320]{2,1,0:T(8,128)(2,1)S(1)}, u32[]{:S(2)}, u32[]{:S(2)}) async-start(bf16[8,320,320]{2,1,0:T(8,128)(2,1)} %regrid.1), calls=%async_computation.1 | async-start | bytes 3932160 | tf_op jit(solution)/shard_map/all_to_all | solution.py:346
  67.1 3.9 %fusion.4 = (f32[64,2560]{1,0:T(8,128)}, f32[64,2560]{1,0:T(8,128)}) fusion(), kind=kLoop, calls=%fused_computation.11 | loop fusion | flops 1474560 | bytes 1310720 | tf_op jit(solution)/shard_map/sin | solution.py:109
  71.0 4.4 %fusion.23 = (f32[10,2,2560]{2,1,0:T(2,128)}, f32[10,2,2560]{2,1,0:T(2,128)}) fusion(s32[10,2]{1,0:T(8,128)S(1)} %copy.54), kind=kLoop, calls=%fused_computation.43 | loop fusion | flops 460800 | bytes 409680 | tf_op jit(solution)/shard_map/sin | solution.py:109
  75.4 13.4 %all-to-all-done.1 = bf16[8,320,320]{2,1,0:T(8,128)(2,1)S(1)} async-done(((bf16[8,320,320]{2,1,0:T(8,128)(2,1)}), bf16[8,320,320]{2,1,0:T(8,128)(2,1)S(1)}, u32[]{:S(2)}, u32[]{:S(2)}) %all-to-all-start.1) | async-done | bytes 1638432 | tf_op jit(solution)/shard_map/all_to_all | solution.py:346
  88.8 1.3 copy-done.1
  90.0 2.7 copy.53
  92.7 2.2 all_to_all.29.rows
  95.0 18.0 %dft.1 = bf16[4,640,320]{2,1,0:T(8,128)(2,1)} custom-call(bf16[320,2560]{1,0:T(8,128)(2,1)} %all_to_all.29.rows, f32[64,2560]{1,0:T(8,128)} %get-tuple-element.25.base_cos, f32[64,2560]{1,0:T(8,128)} %get-tuple-element.24.base_sin, f32[10,2,2560]{2,1,0:T(2,128)} %get-tuple-element.15.step_cos, f32[10,2,2560]{2,1,0:T(2,128)} %get-tuple-element.14.step_sin), custom_call_target="tpu_custom_call" | custom-call | tf_op jit(solution)/shard_map/dft/pallas_call | solution.py:116
  112.9 4.4 %copy.55 = bf16[4,640,320]{2,0,1:T(4,128)(2,1)} copy(bf16[4,640,320]{2,1,0:T(8,128)(2,1)} %dft.1) | data formatting | bytes 3276800 | tf_op jit(solution)/shard_map/dft/pallas_call | solution.py:116
  117.3 5.8 %all-to-all-start.2 = ((bf16[4,640,320]{2,0,1:T(4,128)(2,1)}), bf16[4,640,320]{2,0,1:T(4,128)(2,1)S(1)}, u32[]{:S(2)}, u32[]{:S(2)}) async-start(bf16[4,640,320]{2,0,1:T(4,128)(2,1)} %copy.55), calls=%async_computation.2 | async-start | bytes 3932160 | tf_op jit(solution)/shard_map/all_to_all | solution.py:348
  126.5 42.3 %all-to-all-done.2 = bf16[4,640,320]{2,0,1:T(4,128)(2,1)S(1)} async-done(((bf16[4,640,320]{2,0,1:T(4,128)(2,1)}), bf16[4,640,320]{2,0,1:T(4,128)(2,1)S(1)}, u32[]{:S(2)}, u32[]{:S(2)}) %all-to-all-start.2) | async-done | bytes 1638432 | tf_op jit(solution)/shard_map/all_to_all | solution.py:348
  168.8 2.5 reshape.216
  171.2 2.6 fusion.35
  174.9 5.4 %rev.3 = bf16[8,1,2,2,2,20,320]{6,2,0,4,3,5,1:T(2,128)(2,1)S(1)} reverse(bf16[8,1,2,2,2,20,320]{6,2,0,4,3,5,1:T(2,128)(2,1)S(1)} %copy.59), dimensions={2} | reverse | bytes 1638400 | tf_op jit(solution)/shard_map/rev | solution.py:356
  181.2 2.7 maximum_bitcast_fusion
  184.0 2.4 reshape.217.fields
  186.4 110.8 %legendre.1 = f32[20,16,1281]{2,1,0:T(8,128)} custom-call(s32[1]{0:T(128)} %bitcast.first, bf16[20,64,640]{2,1,0:T(8,128)(2,1)} %reshape.217.fields, f32[1,640]{1,0:T(1,128)} %multiply_cosine_fusion.x_ref, f32[24,640]{1,0:T(8,128)} %get-tuple-element.13.start_low, f32[24,640]{1,0:T(8,128)} %get-tuple-element.12.start_high, ...), custom_call_target="tpu_custom_call" | custom-call | tf_op jit(solution)/shard_map/legendre/pallas_call | solution.py:232
  (57 shorter events, 12.1 us)
Async XLA Ops:
  0.0 2.7 copy-start
  3.3 6.9 %copy-start.3 = (s32[10,1,4]{0,2,1:T(4,128)S(1)}, s32[10,1,4]{0,2,1:T(4,128)}, u32[]{:S(2)}) copy-start(s32[10,1,4]{0,2,1:T(4,128)} %param.10) | copy-start | bytes 484
  3.3 7.1 %copy-start.4 = (s32[10,1,4]{0,2,1:T(4,128)S(1)}, s32[10,1,4]{0,2,1:T(4,128)}, u32[]{:S(2)}) copy-start(s32[10,1,4]{0,2,1:T(4,128)} %param.11) | copy-start | bytes 484
  4.4 25.1 %all-to-all-start = ((bf16[4,3,8,4096]{3,2,1,0:T(8,128)(2,1)}), bf16[4,3,8,4096]{3,2,1,0:T(8,128)(2,1)S(1)}, u32[]{:S(2)}, u32[]{:S(2)}) async-start(bf16[4,3,8,4096]{3,2,1,0:T(8,128)(2,1)} %broadcast_select_fusion), calls=%async_computation | async-start | bytes 1572864 | tf_op jit(solution)/shard_map/all_to_all | solution.py:320
  32.7 2.6 copy-start.2
  61.9 26.9 %all-to-all-start.1 = ((bf16[8,320,320]{2,1,0:T(8,128)(2,1)}), bf16[8,320,320]{2,1,0:T(8,128)(2,1)S(1)}, u32[]{:S(2)}, u32[]{:S(2)}) async-start(bf16[8,320,320]{2,1,0:T(8,128)(2,1)} %regrid.1), calls=%async_computation.1 | async-start | bytes 3932160 | tf_op jit(solution)/shard_map/all_to_all | solution.py:346
  88.8 1.3 copy-start.1
  117.3 51.5 %all-to-all-start.2 = ((bf16[4,640,320]{2,0,1:T(4,128)(2,1)}), bf16[4,640,320]{2,0,1:T(4,128)(2,1)S(1)}, u32[]{:S(2)}, u32[]{:S(2)}) async-start(bf16[4,640,320]{2,0,1:T(4,128)(2,1)} %copy.55), calls=%async_computation.2 | async-start | bytes 3932160 | tf_op jit(solution)/shard_map/all_to_all | solution.py:348

commit v2 on v1

--- a/solution.py
+++ b/solution.py
@@ -19,6 +19,7 @@
 K = 4
 QB = 64
 SB = 128
+AHEAD = 7
 SCALE = 1024.0
 
 
@@ -140,13 +141,8 @@
     return base + step
 
 
-def legendre_kernel(
-    first, fields, x_ref, start_low, start_high, grow, back, out, table, prev_ref, before_ref
-):
-    pairs = out.shape[0]
-    padded = start_low.shape[0]
-    first_pair = first[0]
-    x = x_ref[...]
+def recur(first_pair, x, start_low, start_high, grow, back, table, prev_ref, before_ref, slot0, count):
+    padded = prev_ref.shape[0]
     fresh_last = M - first_pair
     fresh_first = fresh_last - padded + 1
 
@@ -164,83 +160,181 @@
             prev, before = value, prev
         return prev, before
 
-    def block(slot0, count):
-        a_block = grow[:, pl.ds(slot0, SB)]
-        b_block = back[:, pl.ds(slot0, SB)]
-
-        def some(i, carry):
-            prev, before, a8, b8 = carry
-            slot = slot0 + i * 8
-            row = pl.multiple_of(i * 8 * padded, 8)
-            careful = (slot == 0) | ((slot + 7 >= fresh_first) & (slot <= fresh_last))
-            prev, before = lax.cond(
-                careful,
-                lambda p, b: eight(p, b, a8, b8, slot, row, True),
-                lambda p, b: eight(p, b, a8, b8, slot, row, False),
-                prev,
-                before,
-            )
-            return prev, before, pltpu.roll(a8, SB - 8, 1), pltpu.roll(b8, SB - 8, 1)
-
-        carry = (prev_ref[...], before_ref[...], a_block, b_block)
-        prev, before, _, _ = lax.fori_loop(0, count // 8, some, carry)
-        prev_ref[...] = prev
-        before_ref[...] = before
-
-        @pl.loop(0, pairs)
+    def some(i, carry):
+        prev, before, a8, b8 = carry
+        slot = slot0 + i * 8
+        row = pl.multiple_of(i * 8 * padded, 8)
+        careful = (slot == 0) | ((slot + 7 >= fresh_first) & (slot <= fresh_last))
+        prev, before = lax.cond(
+            careful,
+            lambda p, b: eight(p, b, a8, b8, slot, row, True),
+            lambda p, b: eight(p, b, a8, b8, slot, row, False),
+            prev,
+            before,
+        )
+        return prev, before, pltpu.roll(a8, SB - 8, 1), pltpu.roll(b8, SB - 8, 1)
+
+    a_block = grow[:, pl.ds(slot0, SB)]
+    b_block = back[:, pl.ds(slot0, SB)]
+    carry = (prev_ref[...], before_ref[...], a_block, b_block)
+    prev, before, _, _ = lax.fori_loop(0, count // 8, some, carry)
+    prev_ref[...] = prev
+    before_ref[...] = before
+
+
+def split_pair(table, q, count, padded):
+    lanes = [table[lane, pl.ds(q, count, stride=padded), :] for lane in range(HALF // 128)]
+    exact = jnp.concatenate(lanes, axis=1)
+    high = exact.astype(jnp.bfloat16)
+    return high, (exact - high.astype(jnp.float32)).astype(jnp.bfloat16)
+
+
+def unrolled(pairs):
+    return 10 if pairs % 10 == 0 else 5 if pairs % 5 == 0 else 1
+
+
+def ahead_kernel(
+    first, x_ref, start_low, start_high, grow, back, out, prev_ref, before_ref, table
+):
+    pairs = out.shape[1]
+    padded = prev_ref.shape[0]
+    b = pl.program_id(0)
+
+    @pl.when(b == 0)
+    def _():
+        prev_ref[...] = jnp.zeros_like(prev_ref)
+        before_ref[...] = jnp.zeros_like(before_ref)
+
+    slot0 = pl.multiple_of(b * SB, SB)
+    recur(
+        first[0], x_ref[...], start_low, start_high, grow, back, table, prev_ref, before_ref,
+        slot0, SB,
+    )
+
+    @pl.loop(0, pairs, unroll=unrolled(pairs))
+    def _(q):
+        high, low = split_pair(table, q, SB, padded)
+        out[0, q, :, 0:HALF] = high
+        out[0, q, :, HALF : 2 * HALF] = low
+
+
+def ahead(tables, first, pairs):
+    x, start_low, start_high, grow, back = tables
+    padded = start_low.shape[0]
+    full = [pl.BlockSpec(t.shape, lambda b: (0, 0)) for t in tables]
+    state = jax.ShapeDtypeStruct((padded, HALF), jnp.float32)
+    return pl.pallas_call(
+        ahead_kernel,
+        out_shape=(
+            jax.ShapeDtypeStruct((AHEAD, pairs, SB, 2 * HALF), jnp.bfloat16),
+            state,
+            state,
+        ),
+        grid=(AHEAD,),
+        in_specs=[pl.BlockSpec(memory_space=pltpu.SMEM)] + full,
+        out_specs=(
+            pl.BlockSpec((1, pairs, SB, 2 * HALF), lambda b: (b, 0, 0, 0)),
+            pl.BlockSpec((padded, HALF), lambda b: (0, 0)),
+            pl.BlockSpec((padded, HALF), lambda b: (0, 0)),
+        ),
+        scratch_shapes=[pltpu.VMEM((HALF // 128, SB * padded, 128), jnp.float32)],
+        cost_estimate=pl.CostEstimate(
+            flops=40_000_000_000, bytes_accessed=48_000_000, transcendentals=0
+        ),
+        name="ahead",
+    )(first, x, start_low, start_high, grow, back)
+
+
+def legendre_kernel(
+    first, fields, ready, prev_in, before_in, x_ref, start_low, start_high, grow, back, out,
+    table, prev_ref, before_ref,
+):
+    pairs = out.shape[0]
+    padded = prev_ref.shape[0]
+    first_pair = first[0]
+    b = pl.program_id(0)
+    slot0 = pl.multiple_of(b * SB, SB)
+
+    def finish(q, high, low, count):
+        dims = (((1,), (1,)), ((), ()))
+        field = fields[q]
+        sums = lax.dot_general(high, field, dims, preferred_element_type=jnp.float32)
+        sums += lax.dot_general(low, field, dims, preferred_element_type=jnp.float32)
+        sums = sums.T
+        slots = lax.broadcasted_iota(jnp.int32, (2 * LEV, count), 1) + slot0
+        length = M - first_pair - q
+        is_low = slots < length
+        odd = jnp.where(is_low, slots, slots + length) % 2
+        sign = jnp.where(odd == 1, -1.0, 1.0)
+        c = 2 * LEV
+        north = jnp.where(is_low, sums[0:c], sums[2 * c : 3 * c])
+        southern = jnp.where(is_low, sums[c : 2 * c], sums[3 * c : 4 * c])
+        return (north + sign * southern) * (1.0 / SCALE)
+
+    def step(count):
+        recur(
+            first_pair, x_ref[...], start_low, start_high, grow, back, table, prev_ref,
+            before_ref, slot0, count,
+        )
+
+    @pl.when(b == 0)
+    def _():
+        prev_ref[...] = prev_in[...]
+        before_ref[...] = before_in[...]
+
+    @pl.when(b < AHEAD)
+    def _():
+        @pl.loop(0, pairs, unroll=unrolled(pairs))
         def _(q):
-            lanes = [
-                table[lane, pl.ds(q, count, stride=padded), :] for lane in range(HALF // 128)
-            ]
-            p32 = jnp.concatenate(lanes, axis=1)
-            high = p32.astype(jnp.bfloat16)
-            low = (p32 - high.astype(jnp.float32)).astype(jnp.bfloat16)
-            dims = (((1,), (1,)), ((), ()))
-            field = fields[q]
-            sums = lax.dot_general(high, field, dims, preferred_element_type=jnp.float32)
-            sums += lax.dot_general(low, field, dims, preferred_element_type=jnp.float32)
-            sums = sums.T
-            slots = lax.broadcasted_iota(jnp.int32, (2 * LEV, count), 1) + slot0
-            length = M - first_pair - q
-            is_low = slots < length
-            odd = jnp.where(is_low, slots, slots + length) % 2
-            sign = jnp.where(odd == 1, -1.0, 1.0)
-            c = 2 * LEV
-            north = jnp.where(is_low, sums[0:c], sums[2 * c : 3 * c])
-            southern = jnp.where(is_low, sums[c : 2 * c], sums[3 * c : 4 * c])
-            result = (north + sign * southern) * (1.0 / SCALE)
-            if count == SB:
-                out[q, :, pl.ds(slot0, SB)] = result
-            else:
-                out[q, :, M : M + 1] = result[:, 0:1]
-
-    prev_ref[...] = jnp.zeros_like(prev_ref)
-    before_ref[...] = jnp.zeros_like(before_ref)
-
-    @pl.loop(0, M // SB)
-    def _(b):
-        block(pl.multiple_of(b * SB, SB), SB)
-
-    block(M, 8)
-
-
-def legendre(fields, tables, first):
+            high = ready[0, q, :, 0:HALF]
+            low = ready[0, q, :, HALF : 2 * HALF]
+            out[q, :, pl.ds(slot0, SB)] = finish(q, high, low, SB)
+
+    @pl.when((b >= AHEAD) & (b < M // SB))
+    def _():
+        step(SB)
+
+        @pl.loop(0, pairs, unroll=unrolled(pairs))
+        def _(q):
+            high, low = split_pair(table, q, SB, padded)
+            out[q, :, pl.ds(slot0, SB)] = finish(q, high, low, SB)
+
+    @pl.when(b == M // SB)
+    def _():
+        step(8)
+
+        @pl.loop(0, pairs, unroll=unrolled(pairs))
+        def _(q):
+            high, low = split_pair(table, q, 8, padded)
+            out[q, :, M : M + 1] = finish(q, high, low, 8)[:, 0:1]
+
+
+def legendre(fields, tables, first, early):
     x, start_low, start_high, grow, back = tables
+    ready, prev, before = early
     pairs = fields.shape[0]
     padded = start_low.shape[0]
-    vmem = pl.BlockSpec(memory_space=pltpu.VMEM)
+    full = [pl.BlockSpec(t.shape, lambda b: (0, 0)) for t in (prev, before) + tables]
     return pl.pallas_call(
         legendre_kernel,
         out_shape=jax.ShapeDtypeStruct((pairs, 2 * LEV, M + 1), jnp.float32),
-        in_specs=[pl.BlockSpec(memory_space=pltpu.SMEM)] + [vmem] * 6,
-        out_specs=vmem,
+        grid=(M // SB + 1,),
+        in_specs=[
+            pl.BlockSpec(memory_space=pltpu.SMEM),
+            pl.BlockSpec(fields.shape, lambda b: (0, 0, 0)),
+            pl.BlockSpec(
+                (1, pairs, SB, 2 * HALF), lambda b: (jnp.minimum(b, AHEAD - 1), 0, 0, 0)
+            ),
+        ]
+        + full,
+        out_specs=pl.BlockSpec((pairs, 2 * LEV, M + 1), lambda b: (0, 0, 0)),
         scratch_shapes=[
             pltpu.VMEM((HALF // 128, SB * padded, 128), jnp.float32),
             pltpu.VMEM((padded, HALF), jnp.float32),
             pltpu.VMEM((padded, HALF), jnp.float32),
         ],
         name="legendre",
-    )(first, fields, x, start_low, start_high, grow, back)
+    )(first, fields, ready, prev, before, x, start_low, start_high, grow, back)
 
 
 def legendre_tables(first, pairs):
@@ -345,19 +439,23 @@
     flat_rows = field.reshape(LEV * field.shape[1], field.shape[2])
     rows = lax.all_to_all(flat_rows, "tile", split_axis=0, concat_axis=1, tiled=True)
     spectral = dft(rows, dft_tables())
+    pairs = M // 2 // (tile_count * lat_count)
+    first = (tile_me * lat_count + lat_me) * pairs
+    tables = legendre_tables(first, pairs)
+    spectral, x = lax.optimization_barrier((spectral, tables[0]))
+    tables = (x,) + tables[1:]
+    early = ahead(tables, first.reshape(1), pairs)
     arranged = lax.all_to_all(spectral, ("tile", "lat"), split_axis=1, concat_axis=0, tiled=True)
 
     parts = tile_count // LEV
-    pairs = M // 2 // (tile_count * lat_count)
     count = rows.shape[0]
     box = arranged.reshape(LEV, parts, lat_count, 2, 2, pairs, count)
     halves = lat_count // 2
     north = box[:, :, :halves]
-    southern = box[:, :, halves:][:, :, ::-1]
+    southern = jnp.stack([box[:, :, lat_count - 1 - l] for l in range(halves)], axis=2)
     both = jnp.stack([north, southern])
     fields = jnp.transpose(both, (6, 4, 0, 5, 1, 3, 2, 7)).reshape(pairs, 8 * LEV, HALF)
-    first = (tile_me * lat_count + lat_me) * pairs
-    return legendre(fields, legendre_tables(first, pairs), first.reshape(1))
+    return legendre(fields, tables, first.reshape(1), early)
 
 
 def solution(mesh):

time: 298 us -> 226 us (0.76)
  waiting for transfers between devices: 73.1 us -> 29.5 us
  Pallas kernels: 152 us -> 126 us
  local copies, waits for them, and re-layouts: 34.8 us -> 30 us
    pallas_call x1, Pallas kernels: 111 us -> 41.9 us  [legendre(): pl.pallas_call(legendre_kernel, out_shape=jax.ShapeDtypeStruct((pairs, 2...]
    pallas_call x0 -> x1, Pallas kernels: none -> 43.9 us  [ahead(): pl.pallas_call(ahead_kernel, out_shape=(jax.ShapeDtypeStruct((AHEAD, pair...]
    all_to_all x1, waiting for transfers between devices: 42.3 us -> 1.86 us  [whole(): lax.all_to_all(spectral, ('tile', 'lat'), split_axis=1, concat_axis=0, ti...]
    all_to_all x1, waiting for transfers between devices: 17.4 us -> 12 us  [body(): lax.all_to_all(outgoing, 'lat', split_axis=0, concat_axis=0, tiled=True)]
    rev x1 -> x0, local copies, waits for them, and re-layouts: 5.35 us -> none  [whole(): southern = box[:, :, halves:][:, :, ::-1]]
    pallas_call x1 -> x0, local copies, waits for them, and re-layouts: 4.37 us -> none  [dft(): pl.pallas_call(dft_kernel, out_shape=jax.ShapeDtypeStruct((4, M // 2, cou...]
    optimization_barrier x0 -> x1, local copies, waits for them, and re-layouts: none -> 4.36 us  [whole(): spectral, x = lax.optimization_barrier((spectral, tables[0]))]
    unnamed x14 -> x19, local copies, waits for them, and re-layouts: 3.53 us -> 6.1 us
  transfers between devices with their start and end apart: 3 -> 3, of which waited for: 3 -> 3; matrix products, arithmetic and copies ran while one was open for 5% -> 6% of each run, Pallas kernels for 0% -> 19%
where the time goes in v2:
time: 226 us
  Pallas kernels  126 us (56%)
  local copies, waits for them, and re-layouts  30 us (13%)
  waiting for transfers between devices  29.5 us (13%)
  other arithmetic  23.4 us (10%)
  starting transfers between devices  16.3 us (7%)
    pallas_call x1, Pallas kernels, ahead(): pl.pallas_call(ahead_kernel, out_shape=(jax.ShapeDtypeStruct((AHEAD, pair...  43.9 us
    pallas_call x1, Pallas kernels, legendre(): pl.pallas_call(legendre_kernel, out_shape=jax.ShapeDtypeStruct((pairs, 2...  41.9 us
    pallas_call x1, Pallas kernels, regrid(): pl.pallas_call(regrid_kernel, out_shape=jax.ShapeDtypeStruct((LEV, bands...  22.8 us
    pallas_call x1, Pallas kernels, dft(): pl.pallas_call(dft_kernel, out_shape=jax.ShapeDtypeStruct((4, M // 2, cou...  17.9 us
    all_to_all x1, waiting for transfers between devices, whole(): lax.all_to_all(flat_rows, 'tile', split_axis=0, concat_axis=1, tiled=True)  15.6 us
    all_to_all x1, waiting for transfers between devices, body(): lax.all_to_all(outgoing, 'lat', split_axis=0, concat_axis=0, tiled=True)  12 us
    sin x2, other arithmetic, turns(): return (jnp.cos(angle), jnp.sin(angle))  8.22 us
    unnamed x19, local copies, waits for them, and re-layouts  6.1 us
  transfers between devices with their start and end apart: 3, of which 3 were waited for; matrix products, arithmetic and copies ran while one was open for 6% of the time, Pallas kernels for 19%

profile of v2, /device:TPU:1, one launch (start us, length us, event | category | flops | bytes accessed | tf_op | source)
XLA Modules:
  0.0 225.8 jit_solution(14026921495303043924)
XLA Ops:
  4.4 5.4 %all-to-all-start = ((bf16[4,3,8,4096]{3,2,1,0:T(8,128)(2,1)}), bf16[4,3,8,4096]{3,2,1,0:T(8,128)(2,1)S(1)}, u32[]{:S(2)}, u32[]{:S(2)}) async-start(bf16[4,3,8,4096]{3,2,1,0:T(8,128)(2,1)} %broadcast_select_fusion), calls=%async_computation | async-start | bytes 1572864 | tf_op jit(solution)/shard_map/all_to_all | solution.py:414
  13.6 3.8 %fusion.4 = (f32[64,2560]{1,0:T(8,128)}, f32[64,2560]{1,0:T(8,128)}) fusion(), kind=kLoop, calls=%fused_computation.12 | loop fusion | flops 1474560 | bytes 1310720 | tf_op jit(solution)/shard_map/sin | solution.py:110
  17.4 12.0 %all-to-all-done = bf16[4,3,8,4096]{3,2,1,0:T(8,128)(2,1)S(1)} async-done(((bf16[4,3,8,4096]{3,2,1,0:T(8,128)(2,1)}), bf16[4,3,8,4096]{3,2,1,0:T(8,128)(2,1)S(1)}, u32[]{:S(2)}, u32[]{:S(2)}) %all-to-all-start) | async-done | bytes 786464 | tf_op jit(solution)/shard_map/all_to_all | solution.py:414
  29.4 1.7 reshape.216
  31.1 1.6 copy.55
  32.7 2.6 %concatenate.17 = bf16[12,512,64]{2,1,0:T(8,128)(2,1)} reshape(bf16[4,3,8,4096]{3,2,1,0:T(8,128)(2,1)S(1)} %all-to-all-done) | data formatting | bytes 1572864 | tf_op jit(solution)/shard_map/concatenate | solution.py:435
  35.3 3.7 %pad_maximum_fusion.blocks = bf16[24,512,64]{2,1,0:T(8,128)(2,1)} fusion(bf16[12,512,64]{2,1,0:T(8,128)(2,1)S(1)} %bitcast.40, bf16[12,512,64]{2,1,0:T(8,128)(2,1)} %concatenate.17), kind=kLoop, calls=%fused_computation.1 | loop fusion | flops 786432 | bytes 3145728 | tf_op jit(solution)/shard_map/concatenate | solution.py:435
  39.0 22.8 %regrid.1 = bf16[8,320,320]{2,1,0:T(8,128)(2,1)} custom-call(s32[40]{0:T(128)} %select_reduce_fusion.3.pos, s32[40]{0:T(128)} %reshape_squeeze.3.code, s32[1]{0:T(128)} %bitcast.3.south, bf16[24,512,64]{2,1,0:T(8,128)(2,1)} %pad_maximum_fusion.blocks, bf16[10,1,4,32,64]{4,3,2,1,0:T(8,128)(2,1)} %rmap.1, bf16[10,4,64,320]{3,2,1,0:T(8,128)(2,1)} %cmap.1), custom_call_target="tpu_custom_call" | custom-call | tf_op jit(solution)/shard_map/regrid/pallas_call | solution.py:60
  61.8 5.1 %all-to-all-start.1 = ((bf16[8,320,320]{2,1,0:T(8,128)(2,1)}), bf16[8,320,320]{2,1,0:T(8,128)(2,1)S(1)}, u32[]{:S(2)}, u32[]{:S(2)}) async-start(bf16[8,320,320]{2,1,0:T(8,128)(2,1)} %regrid.1), calls=%async_computation.1 | async-start | bytes 3932160 | tf_op jit(solution)/shard_map/all_to_all | solution.py:440
  68.7 4.4 %fusion.23 = (f32[10,2,2560]{2,1,0:T(2,128)}, f32[10,2,2560]{2,1,0:T(2,128)}) fusion(s32[10,2]{1,0:T(8,128)S(1)} %copy.57), kind=kLoop, calls=%fused_computation.44 | loop fusion | flops 460800 | bytes 409680 | tf_op jit(solution)/shard_map/sin | solution.py:110
  73.1 15.6 %all-to-all-done.1 = bf16[8,320,320]{2,1,0:T(8,128)(2,1)S(1)} async-done(((bf16[8,320,320]{2,1,0:T(8,128)(2,1)}), bf16[8,320,320]{2,1,0:T(8,128)(2,1)S(1)}, u32[]{:S(2)}, u32[]{:S(2)}) %all-to-all-start.1) | async-done | bytes 1638432 | tf_op jit(solution)/shard_map/all_to_all | solution.py:440
  90.0 2.7 %copy.56 = bf16[320,8,320]{2,1,0:T(8,128)(2,1)S(1)} copy(bf16[320,8,320]{2,0,1:T(8,128)(2,1)} %bitcast.37) | data formatting | bytes 3276800 | tf_op jit(solution)/shard_map/all_to_all | solution.py:440
  92.7 2.2 all_to_all.29.rows
  94.9 17.9 %dft.1 = bf16[4,640,320]{2,1,0:T(8,128)(2,1)} custom-call(bf16[320,2560]{1,0:T(8,128)(2,1)} %all_to_all.29.rows, f32[64,2560]{1,0:T(8,128)} %get-tuple-element.35.base_cos, f32[64,2560]{1,0:T(8,128)} %get-tuple-element.34.base_sin, f32[10,2,2560]{2,1,0:T(2,128)} %get-tuple-element.25.step_cos, f32[10,2,2560]{2,1,0:T(2,128)} %get-tuple-element.24.step_sin), custom_call_target="tpu_custom_call" | custom-call | tf_op jit(solution)/shard_map/dft/pallas_call | solution.py:117
  112.9 4.4 %copy.58 = bf16[4,640,320]{2,0,1:T(4,128)(2,1)} copy(bf16[4,640,320]{2,1,0:T(8,128)(2,1)} %dft.1) | data formatting | bytes 3276800 | tf_op jit(solution)/shard_map/optimization_barrier | solution.py:445
  117.2 5.7 %all-to-all-start.2 = ((bf16[4,640,320]{2,0,1:T(4,128)(2,1)}), bf16[4,640,320]{2,0,1:T(4,128)(2,1)S(1)}, u32[]{:S(2)}, u32[]{:S(2)}) async-start(bf16[4,640,320]{2,0,1:T(4,128)(2,1)} %copy.58), calls=%async_computation.2 | async-start | bytes 3932160 | tf_op jit(solution)/shard_map/all_to_all | solution.py:448
  123.0 43.9 %ahead.1 = (bf16[7,20,128,1280]{3,2,1,0:T(8,128)(2,1)}, f32[24,640]{1,0:T(8,128)}, f32[24,640]{1,0:T(8,128)}) custom-call(s32[1]{0:T(128)} %bitcast.first, f32[1,640]{1,0:T(1,128)} %multiply_cosine_fusion.x_ref, f32[24,640]{1,0:T(8,128)} %get-tuple-element.23.start_low, f32[24,640]{1,0:T(8,128)} %get-tuple-element.22.start_high, ...), custom_call_target="tpu_custom_call" | custom-call | flops 40000000000 | bytes 48000000 | tf_op jit(solution)/shard_map/ahead/pallas_call | solution.py:226
  166.8 1.9 all-to-all-done.2
  168.7 2.5 %reshape.217 = bf16[8,1,4,2,2,20,320]{6,4,3,5,2,0,1:T(2,128)(2,1)} reshape(bf16[32,4,20,320]{3,1,2,0:T(4,128)(2,1)S(1)} %bitcast.38) | data formatting | bytes 3276800 | tf_op jit(solution)/shard_map/reshape | solution.py:452
  171.2 1.5 copy-done.3
  176.5 2.3 %maximum_bitcast_fusion.1 = bf16[1,8,1,2,2,2,20,320]{7,3,1,5,0,4,6,2:T(2,128)(2,1)S(1)} fusion(bf16[8,1,1,2,2,20,320]{6,2,0,4,3,5,1:T(2,128)(2,1)S(1)} %copy.64, bf16[8,1,1,2,2,20,320]{6,2,0,4,3,5,1:T(2,128)(2,1)S(1)} %copy.63), kind=kLoop, calls=%fused_computation.3 | loop fusion | flops 1638400 | bytes 1638400 | tf_op jit(solution)/shard_map/stack | solution.py:456
  178.9 2.7 %maximum_bitcast_fusion = bf16[20,2,2,2,8,2,1,320]{7,5,4,3,2,1,0,6:T(2,128)(2,1)S(1)} fusion(bf16[1,8,1,2,2,2,20,320]{7,3,1,5,0,4,6,2:T(2,128)(2,1)S(1)} %maximum_bitcast_fusion.1, bf16[1,8,1,2,2,2,20,320]{7,3,1,5,0,4,6,2:T(2,128)(2,1)S(1)} %bitcast.41), kind=kLoop, calls=%fused_computation.2 | loop fusion | flops 819200 | bytes 3276800 | tf_op jit(solution)/shard_map/transpose | solution.py:457
  181.6 2.3 %reshape.218.fields = bf16[20,64,640]{2,1,0:T(8,128)(2,1)} reshape(bf16[20,2,2,2,8,2,1,320]{7,5,4,3,2,1,0,6:T(2,128)(2,1)S(1)} %maximum_bitcast_fusion) | data formatting | bytes 3276800 | tf_op jit(solution)/shard_map/reshape | solution.py:457
  183.9 41.9 %legendre.1 = f32[20,16,1281]{2,1,0:T(8,128)} custom-call(s32[1]{0:T(128)} %bitcast.first, bf16[20,64,640]{2,1,0:T(8,128)(2,1)} %reshape.218.fields, bf16[7,20,128,1280]{3,2,1,0:T(8,128)(2,1)} %get-tuple-element.12.ready, f32[24,640]{1,0:T(8,128)} %get-tuple-element.13.prev_in, f32[24,640]{1,0:T(8,128)} %get-tuple-element.14.before_in, ...), custom_call_target="tpu_custom_call" | custom-call | tf_op jit(solution)/shard_map/legendre/pallas_call | solution.py:318
  (65 shorter events, 14.9 us)
Async XLA Ops:
  0.0 2.7 %copy-start = (bf16[7,8,4096]{2,1,0:T(8,128)(2,1)S(1)}, bf16[7,8,4096]{2,1,0:T(8,128)(2,1)}, u32[]{:S(2)}) copy-start(bf16[7,8,4096]{2,1,0:T(8,128)(2,1)} %param.7) | copy-start | bytes 1376260
  3.3 7.7 %copy-start.5 = (s32[10,1,4]{0,2,1:T(4,128)S(1)}, s32[10,1,4]{0,2,1:T(4,128)}, u32[]{:S(2)}) copy-start(s32[10,1,4]{0,2,1:T(4,128)} %param.10) | copy-start | bytes 484
  3.3 7.9 %copy-start.6 = (s32[10,1,4]{0,2,1:T(4,128)S(1)}, s32[10,1,4]{0,2,1:T(4,128)}, u32[]{:S(2)}) copy-start(s32[10,1,4]{0,2,1:T(4,128)} %param.11) | copy-start | bytes 484
  4.4 25.1 %all-to-all-start = ((bf16[4,3,8,4096]{3,2,1,0:T(8,128)(2,1)}), bf16[4,3,8,4096]{3,2,1,0:T(8,128)(2,1)S(1)}, u32[]{:S(2)}, u32[]{:S(2)}) async-start(bf16[4,3,8,4096]{3,2,1,0:T(8,128)(2,1)} %broadcast_select_fusion), calls=%async_computation | async-start | bytes 1572864 | tf_op jit(solution)/shard_map/all_to_all | solution.py:414
  32.7 2.6 %copy-start.4 = (bf16[12,8,64,64]{3,2,1,0:T(8,128)(2,1)S(1)}, bf16[12,8,64,64]{3,2,1,0:T(8,128)(2,1)}, u32[]{:S(2)}) copy-start(bf16[12,8,64,64]{3,2,1,0:T(8,128)(2,1)} %copy.55) | copy-start | bytes 2359300
  61.8 26.9 %all-to-all-start.1 = ((bf16[8,320,320]{2,1,0:T(8,128)(2,1)}), bf16[8,320,320]{2,1,0:T(8,128)(2,1)S(1)}, u32[]{:S(2)}, u32[]{:S(2)}) async-start(bf16[8,320,320]{2,1,0:T(8,128)(2,1)} %regrid.1), calls=%async_computation.1 | async-start | bytes 3932160 | tf_op jit(solution)/shard_map/all_to_all | solution.py:440
  88.7 1.3 copy-start.2
  117.2 51.5 %all-to-all-start.2 = ((bf16[4,640,320]{2,0,1:T(4,128)(2,1)}), bf16[4,640,320]{2,0,1:T(4,128)(2,1)S(1)}, u32[]{:S(2)}, u32[]{:S(2)}) async-start(bf16[4,640,320]{2,0,1:T(4,128)(2,1)} %copy.58), calls=%async_computation.2 | async-start | bytes 3932160 | tf_op jit(solution)/shard_map/all_to_all | solution.py:448
  171.2 1.5 copy-start.3
  171.2 2.2 slice-start
  183.9 41.9 %copy-start.1 = (bf16[7,8,4096]{2,1,0:T(8,128)(2,1)S(1)}, bf16[7,8,4096]{2,1,0:T(8,128)(2,1)}, u32[]{:S(2)}) copy-start(bf16[7,8,4096]{2,1,0:T(8,128)(2,1)} %param.7) | copy-start | bytes 1376260

commit v3 on v2

--- a/solution.py
+++ b/solution.py
@@ -1,3 +1,4 @@
+import functools
 import math
 
 import jax
@@ -19,7 +20,8 @@
 K = 4
 QB = 64
 SB = 128
-AHEAD = 7
+EARLY = 3
+LATER = 5
 SCALE = 1024.0
 
 
@@ -30,13 +32,13 @@
     return jnp.where(rows == target, 1.0, 0.0).astype(jnp.bfloat16)
 
 
-def regrid_kernel(pos, code, south, blocks, rmap, cmap, out, inner, rall):
+def regrid_kernel(pos, code, south, blocks, turned, rmap, cmap, out, inner, rall):
     g = pl.program_id(0)
     turn = permutation(RB, south[0] == 1)
     for k in range(K):
         c = code[g * K + k]
-        where = pos[g * K + k] + NEED * (c % 2)
-        picked = blocks[where]
+        where = pos[g * K + k]
+        picked = jnp.where(c % 2 == 1, turned[where], blocks[where])
         cols = jnp.dot(permutation(BS, c >= 2), cmap[0, k], preferred_element_type=jnp.float32)
         prod = jnp.dot(picked, cols.astype(jnp.bfloat16), preferred_element_type=jnp.float32)
         inner[:, k * BS : (k + 1) * BS, :] = prod.astype(jnp.bfloat16).reshape(LEV, BS, -1)
@@ -50,7 +52,7 @@
         )
 
 
-def regrid(blocks, rmap, cmap, pos, code, south):
+def regrid(blocks, turned, rmap, cmap, pos, code, south):
     bands = cmap.shape[0]
     width = cmap.shape[3]
 
@@ -64,6 +66,7 @@
             num_scalar_prefetch=3,
             grid=(bands,),
             in_specs=[
+                pl.BlockSpec(blocks.shape, lambda g, *_: (0, 0, 0)),
                 pl.BlockSpec(blocks.shape, lambda g, *_: (0, 0, 0)),
                 pl.BlockSpec((1, 1, K, RB, BS), lambda g, *_: (g, 0, 0, 0, 0)),
                 pl.BlockSpec((1, K, BS, width), lambda g, *_: (g, 0, 0, 0)),
@@ -75,7 +78,7 @@
             ],
         ),
         name="regrid",
-    )(pos, code, south, blocks, rmap, cmap)
+    )(pos, code, south, blocks, turned, rmap, cmap)
 
 
 def dft_kernel(rows, base_cos, base_sin, step_cos, step_sin, out, high, low):
@@ -194,7 +197,7 @@
 
 
 def ahead_kernel(
-    first, x_ref, start_low, start_high, grow, back, out, prev_ref, before_ref, table
+    begin, first, prev_in, before_in, x_ref, start_low, start_high, grow, back, out, prev_ref, before_ref, table
 ):
     pairs = out.shape[1]
     padded = prev_ref.shape[0]
@@ -202,10 +205,10 @@
 
     @pl.when(b == 0)
     def _():
-        prev_ref[...] = jnp.zeros_like(prev_ref)
-        before_ref[...] = jnp.zeros_like(before_ref)
-
-    slot0 = pl.multiple_of(b * SB, SB)
+        prev_ref[...] = prev_in[...]
+        before_ref[...] = before_in[...]
+
+    slot0 = pl.multiple_of((b + begin) * SB, SB)
     recur(
         first[0], x_ref[...], start_low, start_high, grow, back, table, prev_ref, before_ref,
         slot0, SB,
@@ -218,19 +221,19 @@
         out[0, q, :, HALF : 2 * HALF] = low
 
 
-def ahead(tables, first, pairs):
+def ahead(tables, first, pairs, begin, blocks, prev, before):
     x, start_low, start_high, grow, back = tables
     padded = start_low.shape[0]
-    full = [pl.BlockSpec(t.shape, lambda b: (0, 0)) for t in tables]
+    full = [pl.BlockSpec(t.shape, lambda b: (0, 0)) for t in (prev, before) + tables]
     state = jax.ShapeDtypeStruct((padded, HALF), jnp.float32)
     return pl.pallas_call(
-        ahead_kernel,
+        functools.partial(ahead_kernel, begin),
         out_shape=(
-            jax.ShapeDtypeStruct((AHEAD, pairs, SB, 2 * HALF), jnp.bfloat16),
+            jax.ShapeDtypeStruct((blocks, pairs, SB, 2 * HALF), jnp.bfloat16),
             state,
             state,
         ),
-        grid=(AHEAD,),
+        grid=(blocks,),
         in_specs=[pl.BlockSpec(memory_space=pltpu.SMEM)] + full,
         out_specs=(
             pl.BlockSpec((1, pairs, SB, 2 * HALF), lambda b: (b, 0, 0, 0)),
@@ -239,15 +242,15 @@
         ),
         scratch_shapes=[pltpu.VMEM((HALF // 128, SB * padded, 128), jnp.float32)],
         cost_estimate=pl.CostEstimate(
-            flops=40_000_000_000, bytes_accessed=48_000_000, transcendentals=0
+            flops=blocks * 6_000_000_000, bytes_accessed=blocks * 7_000_000, transcendentals=0
         ),
-        name="ahead",
-    )(first, x, start_low, start_high, grow, back)
+        name=f"ahead{begin}",
+    )(first, prev, before, x, start_low, start_high, grow, back)
 
 
 def legendre_kernel(
-    first, fields, ready, prev_in, before_in, x_ref, start_low, start_high, grow, back, out,
-    table, prev_ref, before_ref,
+    width, first, raw, ready, later, prev_in, before_in, x_ref, start_low, start_high, grow, back, out,
+    fields, table, prev_ref, before_ref,
 ):
     pairs = out.shape[0]
     padded = prev_ref.shape[0]
@@ -282,15 +285,35 @@
         prev_ref[...] = prev_in[...]
         before_ref[...] = before_in[...]
 
-    @pl.when(b < AHEAD)
-    def _():
+        @pl.loop(0, pairs)
+        def _(q):
+            c = 2 * LEV
+            for upper in range(2):
+                part = raw[q, upper * c : (upper + 1) * c, :]
+                bands = [
+                    part[:, at : at + width] for at in range(NLAT - width, HALF - 1, -width)
+                ]
+                fields[q, 2 * upper * c : (2 * upper + 1) * c, :] = part[:, 0:HALF]
+                fields[q, (2 * upper + 1) * c : (2 * upper + 2) * c, :] = jnp.concatenate(
+                    bands, axis=1
+                )
+
+    def from_store(store):
         @pl.loop(0, pairs, unroll=unrolled(pairs))
         def _(q):
-            high = ready[0, q, :, 0:HALF]
-            low = ready[0, q, :, HALF : 2 * HALF]
+            high = store[0, q, :, 0:HALF]
+            low = store[0, q, :, HALF : 2 * HALF]
             out[q, :, pl.ds(slot0, SB)] = finish(q, high, low, SB)
 
-    @pl.when((b >= AHEAD) & (b < M // SB))
+    @pl.when(b < EARLY)
+    def _():
+        from_store(ready)
+
+    @pl.when((b >= EARLY) & (b < EARLY + LATER))
+    def _():
+        from_store(later)
+
+    @pl.when((b >= EARLY + LATER) & (b < M // SB))
     def _():
         step(SB)
 
@@ -309,32 +332,37 @@
             out[q, :, M : M + 1] = finish(q, high, low, 8)[:, 0:1]
 
 
-def legendre(fields, tables, first, early):
+def legendre(raw, tables, first, ready, late, width):
     x, start_low, start_high, grow, back = tables
-    ready, prev, before = early
-    pairs = fields.shape[0]
+    later, prev, before = late
+    pairs = raw.shape[0]
     padded = start_low.shape[0]
     full = [pl.BlockSpec(t.shape, lambda b: (0, 0)) for t in (prev, before) + tables]
     return pl.pallas_call(
-        legendre_kernel,
+        functools.partial(legendre_kernel, width),
         out_shape=jax.ShapeDtypeStruct((pairs, 2 * LEV, M + 1), jnp.float32),
         grid=(M // SB + 1,),
         in_specs=[
             pl.BlockSpec(memory_space=pltpu.SMEM),
-            pl.BlockSpec(fields.shape, lambda b: (0, 0, 0)),
+            pl.BlockSpec(raw.shape, lambda b: (0, 0, 0)),
             pl.BlockSpec(
-                (1, pairs, SB, 2 * HALF), lambda b: (jnp.minimum(b, AHEAD - 1), 0, 0, 0)
+                (1, pairs, SB, 2 * HALF), lambda b: (jnp.minimum(b, EARLY - 1), 0, 0, 0)
+            ),
+            pl.BlockSpec(
+                (1, pairs, SB, 2 * HALF),
+                lambda b: (jnp.clip(b - EARLY, 0, LATER - 1), 0, 0, 0),
             ),
         ]
         + full,
         out_specs=pl.BlockSpec((pairs, 2 * LEV, M + 1), lambda b: (0, 0, 0)),
         scratch_shapes=[
+            pltpu.VMEM((pairs, 8 * LEV, HALF), jnp.bfloat16),
             pltpu.VMEM((HALF // 128, SB * padded, 128), jnp.float32),
             pltpu.VMEM((padded, HALF), jnp.float32),
             pltpu.VMEM((padded, HALF), jnp.float32),
         ],
         name="legendre",
-    )(first, fields, ready, prev, before, x, start_low, start_high, grow, back)
+    )(first, raw, ready, later, prev, before, x, start_low, start_high, grow, back)
 
 
 def legendre_tables(first, pairs):
@@ -431,31 +459,31 @@
     wanted = jnp.arange(NEED, dtype=jnp.int32)
     pos = jnp.sum(jnp.where(uses[:, None] == wanted[None, :], place[None, :], 0), axis=1)
     code = codes[:, 0].reshape(-1)
-    pos = pos + (held - NEED) * (code % 2)
-    blocks = jnp.concatenate([flat, jnp.swapaxes(flat, 2, 3)]).reshape(2 * held, LEV * BS, BS)
+    blocks = flat.reshape(held, LEV * BS, BS)
+    turned = jnp.swapaxes(flat, 2, 3).reshape(held, LEV * BS, BS)
     south = (lat_me >= lat_count // 2).astype(jnp.int32).reshape(1)
-    field = regrid(blocks, row_map, col_map, pos, code, south)
+    field = regrid(blocks, turned, row_map, col_map, pos, code, south)
+
+    pairs = M // 2 // (tile_count * lat_count)
+    first = (tile_me * lat_count + lat_me) * pairs
+    tables = legendre_tables(first, pairs)
+    field, x = lax.optimization_barrier((field, tables[0]))
+    tables = (x,) + tables[1:]
+    zeros = jnp.zeros_like(tables[1])
+    ready, prev, before = ahead(tables, first.reshape(1), pairs, 0, EARLY, zeros, zeros)
 
     flat_rows = field.reshape(LEV * field.shape[1], field.shape[2])
     rows = lax.all_to_all(flat_rows, "tile", split_axis=0, concat_axis=1, tiled=True)
     spectral = dft(rows, dft_tables())
-    pairs = M // 2 // (tile_count * lat_count)
-    first = (tile_me * lat_count + lat_me) * pairs
-    tables = legendre_tables(first, pairs)
-    spectral, x = lax.optimization_barrier((spectral, tables[0]))
-    tables = (x,) + tables[1:]
-    early = ahead(tables, first.reshape(1), pairs)
+    spectral, prev = lax.optimization_barrier((spectral, prev))
+    late = ahead(tables, first.reshape(1), pairs, EARLY, LATER, prev, before)
     arranged = lax.all_to_all(spectral, ("tile", "lat"), split_axis=1, concat_axis=0, tiled=True)
 
     parts = tile_count // LEV
     count = rows.shape[0]
     box = arranged.reshape(LEV, parts, lat_count, 2, 2, pairs, count)
-    halves = lat_count // 2
-    north = box[:, :, :halves]
-    southern = jnp.stack([box[:, :, lat_count - 1 - l] for l in range(halves)], axis=2)
-    both = jnp.stack([north, southern])
-    fields = jnp.transpose(both, (6, 4, 0, 5, 1, 3, 2, 7)).reshape(pairs, 8 * LEV, HALF)
-    return legendre(fields, tables, first.reshape(1), early)
+    raw = jnp.transpose(box, (5, 3, 4, 0, 2, 1, 6)).reshape(pairs, 4 * LEV, NLAT)
+    return legendre(raw, tables, first.reshape(1), ready, late, NLAT // lat_count)
 
 
 def solution(mesh):

time: 226 us -> 215 us (0.951)
  waiting for transfers between devices: 29.5 us -> 19 us
  Pallas kernels: 126 us -> 136 us
  other arithmetic: 23.4 us -> 14.7 us
    all_to_all x1, waiting for transfers between devices: 15.6 us -> 0.08 us  [whole(): lax.all_to_all(flat_rows, 'tile', split_axis=0, concat_axis=1, tiled=True)]
    all_to_all x1, waiting for transfers between devices: 1.86 us -> 13.1 us  [whole(): lax.all_to_all(spectral, ('tile', 'lat'), split_axis=1, concat_axis=0, ti...]
    pallas_call x2 -> x3, Pallas kernels: 85.7 us -> 95.7 us  [the longest x2 53.7 us: ahead(): pl.pallas_call(functools.partial(ahead_kernel, begin), out_shape=(jax.Sha...]
    all_to_all x1, waiting for transfers between devices: 12 us -> 5.8 us  [body(): lax.all_to_all(outgoing, 'lat', split_axis=0, concat_axis=0, tiled=True)]
    unnamed x19 -> x12, local copies, waits for them, and re-layouts: 6.1 us -> 1.49 us
    concatenate x1 -> x0, other arithmetic: 3.68 us -> none  [whole(): jnp.concatenate([flat, jnp.swapaxes(flat, 2, 3)])]
    transpose x1 -> x0, other arithmetic: 2.72 us -> none  [whole(): jnp.transpose(both, (6, 4, 0, 5, 1, 3, 2, 7)).reshape(pairs, 8 * LEV, HALF)]
    reshape x1 -> x2, local copies, waits for them, and re-layouts: 2.51 us -> 5.12 us  [whole(): box = arranged.reshape(LEV, parts, lat_count, 2, 2, pairs, count)]
  transfers between devices with their start and end apart: 3 -> 3, of which waited for: 3 -> 3; matrix products, arithmetic and copies ran while one was open for 6% -> 7% of each run, Pallas kernels for 19% -> 25%
where the time goes in v3:
time: 215 us
  Pallas kernels  136 us (63%)
  local copies, waits for them, and re-layouts  28.1 us (13%)
  waiting for transfers between devices  19 us (9%)
  starting transfers between devices  16.4 us (8%)
  other arithmetic  14.7 us (7%)
    pallas_call x2, Pallas kernels, ahead(): pl.pallas_call(functools.partial(ahead_kernel, begin), out_shape=(jax.Sha...  53.7 us
    pallas_call x1, Pallas kernels, legendre(): pl.pallas_call(functools.partial(legendre_kernel, width), out_shape=jax.S...  42 us
    pallas_call x1, Pallas kernels, regrid(): pl.pallas_call(regrid_kernel, out_shape=jax.ShapeDtypeStruct((LEV, bands...  22.8 us
    pallas_call x1, Pallas kernels, dft(): pl.pallas_call(dft_kernel, out_shape=jax.ShapeDtypeStruct((4, M // 2, cou...  17.9 us
    all_to_all x1, waiting for transfers between devices, whole(): lax.all_to_all(spectral, ('tile', 'lat'), split_axis=1, concat_axis=0, ti...  13.1 us
    sin x2, other arithmetic, turns(): return (jnp.cos(angle), jnp.sin(angle))  8.23 us
    all_to_all x1, waiting for transfers between devices, body(): lax.all_to_all(outgoing, 'lat', split_axis=0, concat_axis=0, tiled=True)  5.8 us
    all_to_all x1, starting transfers between devices, whole(): lax.all_to_all(spectral, ('tile', 'lat'), split_axis=1, concat_axis=0, ti...  5.76 us
  transfers between devices with their start and end apart: 3, of which 3 were waited for; matrix products, arithmetic and copies ran while one was open for 7% of the time, Pallas kernels for 25%

profile of v3, /device:TPU:1, one launch (start us, length us, event | category | flops | bytes accessed | tf_op | source)
XLA Modules:
  0.0 214.8 jit_solution(16463967668824494138)
XLA Ops:
  0.8 1.0 select_reduce_fusion.2
  3.3 1.0 broadcast_select_fusion
  4.3 5.5 %all-to-all-start = ((bf16[4,3,8,4096]{3,2,1,0:T(8,128)(2,1)}), bf16[4,3,8,4096]{3,2,1,0:T(8,128)(2,1)S(1)}, u32[]{:S(2)}, u32[]{:S(2)}) async-start(bf16[4,3,8,4096]{3,2,1,0:T(8,128)(2,1)} %broadcast_select_fusion), calls=%async_computation | async-start | bytes 1572864 | tf_op jit(solution)/shard_map/all_to_all | solution.py:442
  10.7 3.8 %fusion.4 = (f32[64,2560]{1,0:T(8,128)}, f32[64,2560]{1,0:T(8,128)}) fusion(), kind=kLoop, calls=%fused_computation.9 | loop fusion | flops 1474560 | bytes 1310720 | tf_op jit(solution)/shard_map/sin | solution.py:113
  19.4 4.4 %fusion.23 = (f32[10,2,2560]{2,1,0:T(2,128)}, f32[10,2,2560]{2,1,0:T(2,128)}) fusion(s32[10,2]{1,0:T(8,128)S(1)} %copy.50), kind=kLoop, calls=%fused_computation.41 | loop fusion | flops 460800 | bytes 409680 | tf_op jit(solution)/shard_map/sin | solution.py:113
  23.8 5.8 %all-to-all-done = bf16[4,3,8,4096]{3,2,1,0:T(8,128)(2,1)S(1)} async-done(((bf16[4,3,8,4096]{3,2,1,0:T(8,128)(2,1)}), bf16[4,3,8,4096]{3,2,1,0:T(8,128)(2,1)S(1)}, u32[]{:S(2)}, u32[]{:S(2)}) %all-to-all-start) | async-done | bytes 786464 | tf_op jit(solution)/shard_map/all_to_all | solution.py:442
  29.6 1.7 reshape.216
  31.3 1.6 copy.48
  32.9 2.6 %reshape_reshape.3.blocks = bf16[12,512,64]{2,1,0:T(8,128)(2,1)} reshape(bf16[4,3,8,4096]{3,2,1,0:T(8,128)(2,1)S(1)} %all-to-all-done) | data formatting | bytes 1572864 | tf_op jit(solution)/shard_map/reshape;reshape | solution.py:462
  35.4 22.8 %regrid.1 = bf16[8,320,320]{2,1,0:T(8,128)(2,1)} custom-call(s32[40]{0:T(128)} %select_reduce_fusion.3.pos, s32[40]{0:T(128)} %reshape_squeeze.3.code, s32[1]{0:T(128)} %bitcast.3.south, bf16[12,512,64]{2,1,0:T(8,128)(2,1)} %reshape_reshape.3.blocks, bf16[12,512,64]{2,1,0:T(8,128)(2,1)} %bitcast.37, bf16[10,1,4,32,64]{4,3,2,1,0:T(8,128)(2,1)} %rmap.1, ...), custom_call_target="tpu_custom_call" | custom-call | tf_op jit(solution)/shard_map/regrid/pallas_call | solution.py:62
  58.3 5.1 %all-to-all-start.1 = ((bf16[8,320,320]{2,1,0:T(8,128)(2,1)}), bf16[8,320,320]{2,1,0:T(8,128)(2,1)S(1)}, u32[]{:S(2)}, u32[]{:S(2)}) async-start(bf16[8,320,320]{2,1,0:T(8,128)(2,1)} %regrid.1), calls=%async_computation.1 | async-start | bytes 3932160 | tf_op jit(solution)/shard_map/all_to_all | solution.py:476
  64.0 21.1 %ahead0.1 = (bf16[3,20,128,1280]{3,2,1,0:T(8,128)(2,1)}, f32[24,640]{1,0:T(8,128)}, f32[24,640]{1,0:T(8,128)}) custom-call(s32[1]{0:T(128)} %bitcast.first, f32[24,640]{1,0:T(8,128)} %broadcast_in_dim.140.prev_in.before_in, f32[24,640]{1,0:T(8,128)} %broadcast_in_dim.140.prev_in.before_in, f32[1,640]{1,0:T(1,128)} %multiply_cosine_fusion.x_ref, ...), custom_call_target="tpu_custom_call" | custom-call | flops 17999998976 | bytes 21000000 | tf_op jit(solution)/shard_map/ahead0/pallas_call | solution.py:229
  85.2 1.3 copy-done.2
  86.5 2.7 %copy.49 = bf16[320,8,320]{2,1,0:T(8,128)(2,1)S(1)} copy(bf16[320,8,320]{2,0,1:T(8,128)(2,1)} %bitcast.34) | data formatting | bytes 3276800 | tf_op jit(solution)/shard_map/all_to_all | solution.py:476
  89.2 2.2 %all_to_all.29.rows = bf16[320,2560]{1,0:T(8,128)(2,1)} reshape(bf16[320,8,320]{2,1,0:T(8,128)(2,1)S(1)} %copy.49) | data formatting | bytes 3276800 | tf_op jit(solution)/shard_map/all_to_all | solution.py:476
  91.4 17.9 %dft.1 = bf16[4,640,320]{2,1,0:T(8,128)(2,1)} custom-call(bf16[320,2560]{1,0:T(8,128)(2,1)} %all_to_all.29.rows, f32[64,2560]{1,0:T(8,128)} %get-tuple-element.43.base_cos, f32[64,2560]{1,0:T(8,128)} %get-tuple-element.42.base_sin, f32[10,2,2560]{2,1,0:T(2,128)} %get-tuple-element.33.step_cos, f32[10,2,2560]{2,1,0:T(2,128)} %get-tuple-element.32.step_sin), custom_call_target="tpu_custom_call" | custom-call | tf_op jit(solution)/shard_map/dft/pallas_call | solution.py:120
  109.3 4.4 %copy.51 = bf16[4,640,320]{2,0,1:T(4,128)(2,1)} copy(bf16[4,640,320]{2,1,0:T(8,128)(2,1)} %dft.1) | data formatting | bytes 3276800 | tf_op jit(solution)/shard_map/optimization_barrier | solution.py:478
  113.7 5.8 %all-to-all-start.2 = ((bf16[4,640,320]{2,0,1:T(4,128)(2,1)}), bf16[4,640,320]{2,0,1:T(4,128)(2,1)S(1)}, u32[]{:S(2)}, u32[]{:S(2)}) async-start(bf16[4,640,320]{2,0,1:T(4,128)(2,1)} %copy.51), calls=%async_computation.2 | async-start | bytes 3932160 | tf_op jit(solution)/shard_map/all_to_all | solution.py:480
  119.5 32.6 %ahead3.1 = (bf16[5,20,128,1280]{3,2,1,0:T(8,128)(2,1)}, f32[24,640]{1,0:T(8,128)}, f32[24,640]{1,0:T(8,128)}) custom-call(s32[1]{0:T(128)} %bitcast.first, f32[24,640]{1,0:T(8,128)} %get-tuple-element.20.prev_in, f32[24,640]{1,0:T(8,128)} %get-tuple-element.21.before_in, f32[1,640]{1,0:T(1,128)} %multiply_cosine_fusion.x_ref, ...), custom_call_target="tpu_custom_call" | custom-call | flops 30000001024 | bytes 35000000 | tf_op jit(solution)/shard_map/ahead3/pallas_call | solution.py:229
  152.1 13.1 %all-to-all-done.2 = bf16[4,640,320]{2,0,1:T(4,128)(2,1)S(1)} async-done(((bf16[4,640,320]{2,0,1:T(4,128)(2,1)}), bf16[4,640,320]{2,0,1:T(4,128)(2,1)S(1)}, u32[]{:S(2)}, u32[]{:S(2)}) %all-to-all-start.2) | async-done | bytes 1638432 | tf_op jit(solution)/shard_map/all_to_all | solution.py:480
  165.2 2.5 %reshape.220 = bf16[8,1,4,2,2,20,320]{6,4,3,5,2,0,1:T(2,128)(2,1)} reshape(bf16[32,4,20,320]{3,1,2,0:T(4,128)(2,1)S(1)} %bitcast.35) | data formatting | bytes 3276800 | tf_op jit(solution)/shard_map/reshape | solution.py:484
  167.7 2.6 %copy.54 = bf16[8,1,4,2,2,20,320]{6,2,0,4,3,5,1:T(4,128)(2,1)S(1)} copy(bf16[8,1,4,2,2,20,320]{6,4,3,5,2,0,1:T(2,128)(2,1)} %reshape.220) | data formatting | bytes 3276800 | tf_op jit(solution)/shard_map/reshape | solution.py:484
  170.3 2.4 %reshape.221.raw = bf16[20,32,1280]{2,1,0:T(8,128)(2,1)} reshape(bf16[20,2,2,8,4,1,320]{6,4,3,2,1,0,5:T(4,128)(2,1)S(1)} %bitcast.33) | data formatting | bytes 3276800 | tf_op jit(solution)/shard_map/reshape | solution.py:485
  172.8 42.0 %legendre.1 = f32[20,16,1281]{2,1,0:T(8,128)} custom-call(s32[1]{0:T(128)} %bitcast.first, bf16[20,32,1280]{2,1,0:T(8,128)(2,1)} %reshape.221.raw, bf16[3,20,128,1280]{3,2,1,0:T(8,128)(2,1)} %get-tuple-element.19.ready, bf16[5,20,128,1280]{3,2,1,0:T(8,128)(2,1)} %get-tuple-element.22.later, f32[24,640]{1,0:T(8,128)} %get-tuple-element.23.prev_in, ...), custom_call_target="tpu_custom_call" | custom-call | tf_op jit(solution)/shard_map/legendre/pallas_call | solution.py:341
  (55 shorter events, 8.5 us)
Async XLA Ops:
  0.0 2.7 %copy-start = (bf16[7,8,4096]{2,1,0:T(8,128)(2,1)S(1)}, bf16[7,8,4096]{2,1,0:T(8,128)(2,1)}, u32[]{:S(2)}) copy-start(bf16[7,8,4096]{2,1,0:T(8,128)(2,1)} %param.7) | copy-start | bytes 1376260
  3.3 11.2 %copy-start.3 = (s32[10,1,4]{0,2,1:T(4,128)S(1)}, s32[10,1,4]{0,2,1:T(4,128)}, u32[]{:S(2)}) copy-start(s32[10,1,4]{0,2,1:T(4,128)} %param.10) | copy-start | bytes 484
  4.3 13.4 %copy-start.4 = (s32[10,1,4]{0,2,1:T(4,128)S(1)}, s32[10,1,4]{0,2,1:T(4,128)}, u32[]{:S(2)}) copy-start(s32[10,1,4]{0,2,1:T(4,128)} %param.11) | copy-start | bytes 484
  4.3 25.2 %all-to-all-start = ((bf16[4,3,8,4096]{3,2,1,0:T(8,128)(2,1)}), bf16[4,3,8,4096]{3,2,1,0:T(8,128)(2,1)S(1)}, u32[]{:S(2)}, u32[]{:S(2)}) async-start(bf16[4,3,8,4096]{3,2,1,0:T(8,128)(2,1)} %broadcast_select_fusion), calls=%async_computation | async-start | bytes 1572864 | tf_op jit(solution)/shard_map/all_to_all | solution.py:442
  58.3 26.9 %all-to-all-start.1 = ((bf16[8,320,320]{2,1,0:T(8,128)(2,1)}), bf16[8,320,320]{2,1,0:T(8,128)(2,1)S(1)}, u32[]{:S(2)}, u32[]{:S(2)}) async-start(bf16[8,320,320]{2,1,0:T(8,128)(2,1)} %regrid.1), calls=%async_computation.1 | async-start | bytes 3932160 | tf_op jit(solution)/shard_map/all_to_all | solution.py:476
  85.2 1.3 copy-start.2
  113.7 51.5 %all-to-all-start.2 = ((bf16[4,640,320]{2,0,1:T(4,128)(2,1)}), bf16[4,640,320]{2,0,1:T(4,128)(2,1)S(1)}, u32[]{:S(2)}, u32[]{:S(2)}) async-start(bf16[4,640,320]{2,0,1:T(4,128)(2,1)} %copy.51), calls=%async_computation.2 | async-start | bytes 3932160 | tf_op jit(solution)/shard_map/all_to_all | solution.py:480
  172.8 42.0 %copy-start.1 = (bf16[7,8,4096]{2,1,0:T(8,128)(2,1)S(1)}, bf16[7,8,4096]{2,1,0:T(8,128)(2,1)}, u32[]{:S(2)}) copy-start(bf16[7,8,4096]{2,1,0:T(8,128)(2,1)} %param.7) | copy-start | bytes 1376260

commit v4 on v3

--- a/solution.py
+++ b/solution.py
@@ -193,7 +193,7 @@
 
 
 def unrolled(pairs):
-    return 10 if pairs % 10 == 0 else 5 if pairs % 5 == 0 else 1
+    return 20 if pairs % 20 == 0 else 5 if pairs % 5 == 0 else 1
 
 
 def ahead_kernel(
@@ -285,7 +285,7 @@
         prev_ref[...] = prev_in[...]
         before_ref[...] = before_in[...]
 
-        @pl.loop(0, pairs)
+        @pl.loop(0, pairs, unroll=unrolled(pairs))
         def _(q):
             c = 2 * LEV
             for upper in range(2):

time: 215 us -> 213 us (level)
  Pallas kernels: 136 us -> 133 us
    pallas_call x1, Pallas kernels: 42 us -> 39.1 us  [legendre(): pl.pallas_call(functools.partial(legendre_kernel, width), out_shape=jax.S...]
where the time goes in v4:
time: 213 us; the launch traced here: 212 us
  Pallas kernels  133 us (62%)
  local copies, waits for them, and re-layouts  28.1 us (13%)
  waiting for transfers between devices  19.2 us (9%)
  starting transfers between devices  16.4 us (8%)
  other arithmetic  14.7 us (7%)
    pallas_call x2, Pallas kernels, ahead(): pl.pallas_call(functools.partial(ahead_kernel, begin), out_shape=(jax.Sha...  53.4 us
    pallas_call x1, Pallas kernels, legendre(): pl.pallas_call(functools.partial(legendre_kernel, width), out_shape=jax.S...  39.1 us
    pallas_call x1, Pallas kernels, regrid(): pl.pallas_call(regrid_kernel, out_shape=jax.ShapeDtypeStruct((LEV, bands...  22.8 us
    pallas_call x1, Pallas kernels, dft(): pl.pallas_call(dft_kernel, out_shape=jax.ShapeDtypeStruct((4, M // 2, cou...  17.9 us
    all_to_all x1, waiting for transfers between devices, whole(): lax.all_to_all(spectral, ('tile', 'lat'), split_axis=1, concat_axis=0, ti...  13.3 us
    sin x2, other arithmetic, turns(): return (jnp.cos(angle), jnp.sin(angle))  8.23 us
    all_to_all x1, waiting for transfers between devices, body(): lax.all_to_all(outgoing, 'lat', split_axis=0, concat_axis=0, tiled=True)  5.8 us
    all_to_all x1, starting transfers between devices, whole(): lax.all_to_all(spectral, ('tile', 'lat'), split_axis=1, concat_axis=0, ti...  5.76 us
  transfers between devices with their start and end apart: 3, of which 3 were waited for; matrix products, arithmetic and copies ran while one was open for 7% of the time, Pallas kernels for 25%

profile of v4, /device:TPU:1, one launch (start us, length us, event | category | flops | bytes accessed | tf_op | source)
XLA Modules:
  0.0 211.9 jit_solution(16940671635238563514)
XLA Ops:
  0.8 1.0 select_reduce_fusion.2
  3.3 1.0 broadcast_select_fusion
  4.3 5.5 %all-to-all-start = ((bf16[4,3,8,4096]{3,2,1,0:T(8,128)(2,1)}), bf16[4,3,8,4096]{3,2,1,0:T(8,128)(2,1)S(1)}, u32[]{:S(2)}, u32[]{:S(2)}) async-start(bf16[4,3,8,4096]{3,2,1,0:T(8,128)(2,1)} %broadcast_select_fusion), calls=%async_computation | async-start | bytes 1572864 | tf_op jit(solution)/shard_map/all_to_all | solution.py:442
  10.7 3.8 %fusion.4 = (f32[64,2560]{1,0:T(8,128)}, f32[64,2560]{1,0:T(8,128)}) fusion(), kind=kLoop, calls=%fused_computation.9 | loop fusion | flops 1474560 | bytes 1310720 | tf_op jit(solution)/shard_map/sin | solution.py:113
  19.4 4.4 %fusion.23 = (f32[10,2,2560]{2,1,0:T(2,128)}, f32[10,2,2560]{2,1,0:T(2,128)}) fusion(s32[10,2]{1,0:T(8,128)S(1)} %copy.50), kind=kLoop, calls=%fused_computation.41 | loop fusion | flops 460800 | bytes 409680 | tf_op jit(solution)/shard_map/sin | solution.py:113
  23.8 5.8 %all-to-all-done = bf16[4,3,8,4096]{3,2,1,0:T(8,128)(2,1)S(1)} async-done(((bf16[4,3,8,4096]{3,2,1,0:T(8,128)(2,1)}), bf16[4,3,8,4096]{3,2,1,0:T(8,128)(2,1)S(1)}, u32[]{:S(2)}, u32[]{:S(2)}) %all-to-all-start) | async-done | bytes 786464 | tf_op jit(solution)/shard_map/all_to_all | solution.py:442
  29.6 1.7 reshape.216
  31.3 1.6 copy.48
  32.9 2.6 %reshape_reshape.3.blocks = bf16[12,512,64]{2,1,0:T(8,128)(2,1)} reshape(bf16[4,3,8,4096]{3,2,1,0:T(8,128)(2,1)S(1)} %all-to-all-done) | data formatting | bytes 1572864 | tf_op jit(solution)/shard_map/reshape;reshape | solution.py:462
  35.4 22.8 %regrid.1 = bf16[8,320,320]{2,1,0:T(8,128)(2,1)} custom-call(s32[40]{0:T(128)} %select_reduce_fusion.3.pos, s32[40]{0:T(128)} %reshape_squeeze.3.code, s32[1]{0:T(128)} %bitcast.3.south, bf16[12,512,64]{2,1,0:T(8,128)(2,1)} %reshape_reshape.3.blocks, bf16[12,512,64]{2,1,0:T(8,128)(2,1)} %bitcast.37, bf16[10,1,4,32,64]{4,3,2,1,0:T(8,128)(2,1)} %rmap.1, ...), custom_call_target="tpu_custom_call" | custom-call | tf_op jit(solution)/shard_map/regrid/pallas_call | solution.py:62
  58.3 5.1 %all-to-all-start.1 = ((bf16[8,320,320]{2,1,0:T(8,128)(2,1)}), bf16[8,320,320]{2,1,0:T(8,128)(2,1)S(1)}, u32[]{:S(2)}, u32[]{:S(2)}) async-start(bf16[8,320,320]{2,1,0:T(8,128)(2,1)} %regrid.1), calls=%async_computation.1 | async-start | bytes 3932160 | tf_op jit(solution)/shard_map/all_to_all | solution.py:476
  64.0 21.0 %ahead0.1 = (bf16[3,20,128,1280]{3,2,1,0:T(8,128)(2,1)}, f32[24,640]{1,0:T(8,128)}, f32[24,640]{1,0:T(8,128)}) custom-call(s32[1]{0:T(128)} %bitcast.first, f32[24,640]{1,0:T(8,128)} %broadcast_in_dim.140.prev_in.before_in, f32[24,640]{1,0:T(8,128)} %broadcast_in_dim.140.prev_in.before_in, f32[1,640]{1,0:T(1,128)} %multiply_cosine_fusion.x_ref, ...), custom_call_target="tpu_custom_call" | custom-call | flops 17999998976 | bytes 21000000 | tf_op jit(solution)/shard_map/ahead0/pallas_call | solution.py:229
  85.2 1.3 copy-done.2
  86.5 2.7 %copy.49 = bf16[320,8,320]{2,1,0:T(8,128)(2,1)S(1)} copy(bf16[320,8,320]{2,0,1:T(8,128)(2,1)} %bitcast.34) | data formatting | bytes 3276800 | tf_op jit(solution)/shard_map/all_to_all | solution.py:476
  89.2 2.2 %all_to_all.29.rows = bf16[320,2560]{1,0:T(8,128)(2,1)} reshape(bf16[320,8,320]{2,1,0:T(8,128)(2,1)S(1)} %copy.49) | data formatting | bytes 3276800 | tf_op jit(solution)/shard_map/all_to_all | solution.py:476
  91.4 17.9 %dft.1 = bf16[4,640,320]{2,1,0:T(8,128)(2,1)} custom-call(bf16[320,2560]{1,0:T(8,128)(2,1)} %all_to_all.29.rows, f32[64,2560]{1,0:T(8,128)} %get-tuple-element.43.base_cos, f32[64,2560]{1,0:T(8,128)} %get-tuple-element.42.base_sin, f32[10,2,2560]{2,1,0:T(2,128)} %get-tuple-element.33.step_cos, f32[10,2,2560]{2,1,0:T(2,128)} %get-tuple-element.32.step_sin), custom_call_target="tpu_custom_call" | custom-call | tf_op jit(solution)/shard_map/dft/pallas_call | solution.py:120
  109.3 4.4 %copy.51 = bf16[4,640,320]{2,0,1:T(4,128)(2,1)} copy(bf16[4,640,320]{2,1,0:T(8,128)(2,1)} %dft.1) | data formatting | bytes 3276800 | tf_op jit(solution)/shard_map/optimization_barrier | solution.py:478
  113.7 5.8 %all-to-all-start.2 = ((bf16[4,640,320]{2,0,1:T(4,128)(2,1)}), bf16[4,640,320]{2,0,1:T(4,128)(2,1)S(1)}, u32[]{:S(2)}, u32[]{:S(2)}) async-start(bf16[4,640,320]{2,0,1:T(4,128)(2,1)} %copy.51), calls=%async_computation.2 | async-start | bytes 3932160 | tf_op jit(solution)/shard_map/all_to_all | solution.py:480
  119.5 32.5 %ahead3.1 = (bf16[5,20,128,1280]{3,2,1,0:T(8,128)(2,1)}, f32[24,640]{1,0:T(8,128)}, f32[24,640]{1,0:T(8,128)}) custom-call(s32[1]{0:T(128)} %bitcast.first, f32[24,640]{1,0:T(8,128)} %get-tuple-element.20.prev_in, f32[24,640]{1,0:T(8,128)} %get-tuple-element.21.before_in, f32[1,640]{1,0:T(1,128)} %multiply_cosine_fusion.x_ref, ...), custom_call_target="tpu_custom_call" | custom-call | flops 30000001024 | bytes 35000000 | tf_op jit(solution)/shard_map/ahead3/pallas_call | solution.py:229
  151.9 13.3 %all-to-all-done.2 = bf16[4,640,320]{2,0,1:T(4,128)(2,1)S(1)} async-done(((bf16[4,640,320]{2,0,1:T(4,128)(2,1)}), bf16[4,640,320]{2,0,1:T(4,128)(2,1)S(1)}, u32[]{:S(2)}, u32[]{:S(2)}) %all-to-all-start.2) | async-done | bytes 1638432 | tf_op jit(solution)/shard_map/all_to_all | solution.py:480
  165.2 2.5 %reshape.220 = bf16[8,1,4,2,2,20,320]{6,4,3,5,2,0,1:T(2,128)(2,1)} reshape(bf16[32,4,20,320]{3,1,2,0:T(4,128)(2,1)S(1)} %bitcast.35) | data formatting | bytes 3276800 | tf_op jit(solution)/shard_map/reshape | solution.py:484
  167.7 2.6 %copy.54 = bf16[8,1,4,2,2,20,320]{6,2,0,4,3,5,1:T(4,128)(2,1)S(1)} copy(bf16[8,1,4,2,2,20,320]{6,4,3,5,2,0,1:T(2,128)(2,1)} %reshape.220) | data formatting | bytes 3276800 | tf_op jit(solution)/shard_map/reshape | solution.py:484
  170.3 2.4 %reshape.221.raw = bf16[20,32,1280]{2,1,0:T(8,128)(2,1)} reshape(bf16[20,2,2,8,4,1,320]{6,4,3,2,1,0,5:T(4,128)(2,1)S(1)} %bitcast.33) | data formatting | bytes 3276800 | tf_op jit(solution)/shard_map/reshape | solution.py:485
  172.8 39.1 %legendre.1 = f32[20,16,1281]{2,1,0:T(8,128)} custom-call(s32[1]{0:T(128)} %bitcast.first, bf16[20,32,1280]{2,1,0:T(8,128)(2,1)} %reshape.221.raw, bf16[3,20,128,1280]{3,2,1,0:T(8,128)(2,1)} %get-tuple-element.19.ready, bf16[5,20,128,1280]{3,2,1,0:T(8,128)(2,1)} %get-tuple-element.22.later, f32[24,640]{1,0:T(8,128)} %get-tuple-element.23.prev_in, ...), custom_call_target="tpu_custom_call" | custom-call | tf_op jit(solution)/shard_map/legendre/pallas_call | solution.py:341
  (55 shorter events, 8.6 us)
Async XLA Ops:
  0.0 2.7 %copy-start = (bf16[7,8,4096]{2,1,0:T(8,128)(2,1)S(1)}, bf16[7,8,4096]{2,1,0:T(8,128)(2,1)}, u32[]{:S(2)}) copy-start(bf16[7,8,4096]{2,1,0:T(8,128)(2,1)} %param.7) | copy-start | bytes 1376260
  3.3 11.2 %copy-start.3 = (s32[10,1,4]{0,2,1:T(4,128)S(1)}, s32[10,1,4]{0,2,1:T(4,128)}, u32[]{:S(2)}) copy-start(s32[10,1,4]{0,2,1:T(4,128)} %param.10) | copy-start | bytes 484
  4.3 13.4 %copy-start.4 = (s32[10,1,4]{0,2,1:T(4,128)S(1)}, s32[10,1,4]{0,2,1:T(4,128)}, u32[]{:S(2)}) copy-start(s32[10,1,4]{0,2,1:T(4,128)} %param.11) | copy-start | bytes 484
  4.3 25.2 %all-to-all-start = ((bf16[4,3,8,4096]{3,2,1,0:T(8,128)(2,1)}), bf16[4,3,8,4096]{3,2,1,0:T(8,128)(2,1)S(1)}, u32[]{:S(2)}, u32[]{:S(2)}) async-start(bf16[4,3,8,4096]{3,2,1,0:T(8,128)(2,1)} %broadcast_select_fusion), calls=%async_computation | async-start | bytes 1572864 | tf_op jit(solution)/shard_map/all_to_all | solution.py:442
  58.3 26.9 %all-to-all-start.1 = ((bf16[8,320,320]{2,1,0:T(8,128)(2,1)}), bf16[8,320,320]{2,1,0:T(8,128)(2,1)S(1)}, u32[]{:S(2)}, u32[]{:S(2)}) async-start(bf16[8,320,320]{2,1,0:T(8,128)(2,1)} %regrid.1), calls=%async_computation.1 | async-start | bytes 3932160 | tf_op jit(solution)/shard_map/all_to_all | solution.py:476
  85.2 1.3 copy-start.2
  113.7 51.5 %all-to-all-start.2 = ((bf16[4,640,320]{2,0,1:T(4,128)(2,1)}), bf16[4,640,320]{2,0,1:T(4,128)(2,1)S(1)}, u32[]{:S(2)}, u32[]{:S(2)}) async-start(bf16[4,640,320]{2,0,1:T(4,128)(2,1)} %copy.51), calls=%async_computation.2 | async-start | bytes 3932160 | tf_op jit(solution)/shard_map/all_to_all | solution.py:480
  172.8 39.1 %copy-start.1 = (bf16[7,8,4096]{2,1,0:T(8,128)(2,1)S(1)}, bf16[7,8,4096]{2,1,0:T(8,128)(2,1)}, u32[]{:S(2)}) copy-start(bf16[7,8,4096]{2,1,0:T(8,128)(2,1)} %param.7) | copy-start | bytes 1376260
